TPU v7x, 32 devices: a whole 2x2x4 slice. The times are simulated.
32 devices in a mesh: wide: 8 (over y, x, core), narrow: 4 (over z).
Axes of the slice: x: 2, y: 2, z: 4, core: 2. Of those that a mesh axis runs over, the one named last changes fastest.
Arguments:
- layer_in: bfloat16 [16384, 1024], P(('wide', 'narrow')), may hold values from -6 to 6
- value_first: bfloat16 [16384, 1024], P(('wide', 'narrow')), may hold values from -16 to 16
- seg_start: int32 [16], P('wide'), may hold values from 0 to 1, as said below
- gain_one: float32 [1024], replicated, may hold values from 0.5 to 1.5
- w_qkv: bfloat16 [3, 1024, 1024], P(None, 'narrow'), may hold values from -0.1875 to 0.1875
- w_out: bfloat16 [1024, 1024], P('narrow'), may hold values from -0.75 to 0.75
- gain_two: float32 [1024], replicated, may hold values from 0.5 to 1.5
- w_mlp: bfloat16 [1024, 3, 2816], P('wide', None, 'narrow'), may hold values from -0.1875 to 0.1875
- grad_out: bfloat16 [16384, 1024], P(('wide', 'narrow')), may hold values from -6 to 6
Outputs:
- layer_out: bfloat16 [16384, 1024], P(('wide', 'narrow'))
- grad_in: float32 [16384, 1024], P(('wide', 'narrow'))
- grad_value_first: float32 [16384, 1024], P(('wide', 'narrow'))
- grad_gain_one: float32 [1024], replicated
- grad_w_qkv: float32 [3, 1024, 1024], P(None, 'narrow')
- grad_w_out: float32 [1024, 1024], P('narrow')
- grad_gain_two: float32 [1024], replicated
- grad_w_mlp: float32 [1024, 3, 2816], P('wide', None, 'narrow')
- value_norms: float32 [2], replicated
Inputs may be any that keep to these rules, and one draw needn't show every extreme that they name: `seg_start`: every packed row of 2 slots begins with 1, and a 0 follows only a 1, so each sequence fills one or two slots.
All inputs are finite; a program needn't handle non-finite values.
Results may differ from a plain program's by a relative error of at most 0.014.
Values may be sent and summed in bfloat16 or wider, within the bound.
A program may use at most 192 MiB of HBM per device.

v0:
```python
import jax
import jax.numpy as jnp
from jax import lax
from jax.sharding import PartitionSpec as P

HEAD_DIM = 64


EPSILON = 1e-06


def product(left_side, right_side):
    return jnp.dot(left_side, right_side, preferred_element_type=jnp.float32)


def contract_rows(left_side, right_side):
    return lax.dot_general(
        left_side, right_side, (((0,), (0,)), ((), ())), preferred_element_type=jnp.float32
    )


def contract_cols(left_side, right_side):
    return lax.dot_general(
        left_side, right_side, (((1,), (1,)), ((), ())), preferred_element_type=jnp.float32
    )


def rope_tables(positions):
    half_dim = HEAD_DIM // 2
    frequency = 10000.0 ** (-2.0 * jnp.arange(half_dim, dtype=jnp.float32) / HEAD_DIM)
    angles = positions[:, None] * frequency[None, :]
    return (jnp.cos(angles), jnp.sin(angles))


def rotate(heads_in, cosine, sine_vals):
    half_dim = heads_in.shape[-1] // 2
    first_half = heads_in[..., :half_dim]
    second_half = heads_in[..., half_dim:]
    cos_wide = cosine[:, None, :]
    sin_wide = sine_vals[:, None, :]
    return jnp.concatenate(
        [
            first_half * cos_wide - second_half * sin_wide,
            second_half * cos_wide + first_half * sin_wide,
        ],
        axis=-1,
    )


def gather_rows(values):
    return lax.all_gather(values, "narrow", axis=0, tiled=True)


def narrow_sum(values):
    return lax.psum_scatter(values, "narrow", scatter_dimension=0, tiled=True)


def head_sum(values):
    return lax.psum_scatter(values, "narrow", scatter_dimension=0, tiled=True)


def gather_full(values):
    return lax.all_gather(values, "narrow", axis=0, tiled=True)


def window_scores(
    query_vals, key_vals, mixed_vals, seg_tok, block_index, block_len, span_len, key_start
):
    q_start = block_index * block_len
    q_block = lax.dynamic_slice_in_dim(query_vals, q_start, block_len, 0)
    k_block = lax.dynamic_slice_in_dim(key_vals, key_start, span_len, 0)
    v_block = lax.dynamic_slice_in_dim(mixed_vals, key_start, span_len, 0)
    q_seg = lax.dynamic_slice_in_dim(seg_tok, q_start, block_len, 0)
    k_seg = lax.dynamic_slice_in_dim(seg_tok, key_start, span_len, 0)
    q_place = q_start + jnp.arange(block_len, dtype=jnp.int32)
    k_place = key_start + jnp.arange(span_len, dtype=jnp.int32)
    allowed = (k_place[None, :] <= q_place[:, None]) & (k_seg[None, :] == q_seg[:, None])
    scores = jnp.einsum(
        "qhd,khd->hqk", q_block, k_block, preferred_element_type=jnp.float32
    ) * HEAD_DIM ** (-0.5)
    scores = jnp.where(allowed[None], scores, -1e30)
    return (scores, q_block, k_block, v_block)


def attend_forward(query_vals, key_vals, mixed_vals, seg_start, seg_tok, short_len):
    row_count, head_count, head_dim = query_vals.shape
    block_len = min(512, short_len)
    per_slot = short_len // block_len

    def span_forward(block_index, span_len, key_start):
        scores, q_block, k_block, v_block = window_scores(
            query_vals, key_vals, mixed_vals, seg_tok, block_index, block_len, span_len, key_start
        )
        row_max = jnp.max(scores, axis=-1, keepdims=True)
        exponent = jnp.exp(scores - row_max)
        totals = jnp.sum(exponent, axis=-1, keepdims=True)
        weights = (exponent / totals).astype(jnp.bfloat16)
        outputs = jnp.einsum("hqk,khd->qhd", weights, v_block, preferred_element_type=jnp.float32)
        return (outputs, (row_max + jnp.log(totals))[:, :, 0])

    def block_step(block_index, carried):
        outputs, log_sums = carried
        slot_index = block_index // per_slot
        own_start = slot_index * short_len
        wide_start = jnp.maximum(slot_index - 1, 0) * short_len
        result, log_sum = lax.cond(
            seg_start[slot_index] == 1,
            lambda: span_forward(block_index, short_len, own_start),
            lambda: span_forward(block_index, 2 * short_len, wide_start),
        )
        outputs = lax.dynamic_update_slice_in_dim(outputs, result, block_index * block_len, 0)
        log_sums = lax.dynamic_update_slice_in_dim(log_sums, log_sum, block_index * block_len, 1)
        return (outputs, log_sums)

    initial = (
        jnp.zeros((row_count, head_count, head_dim), jnp.float32),
        jnp.zeros((head_count, row_count), jnp.float32),
    )
    return lax.fori_loop(0, row_count // block_len, block_step, initial)


def attend_backward(
    query_vals, key_vals, mixed_vals, grad_att, log_sums, seg_start, seg_tok, short_len
):
    row_count, head_count, head_dim = query_vals.shape
    block_len = min(512, short_len)
    per_slot = short_len // block_len
    scale = HEAD_DIM ** (-0.5)

    def span_backward(block_index, span_len, key_start):
        scores, q_block, k_block, v_block = window_scores(
            query_vals, key_vals, mixed_vals, seg_tok, block_index, block_len, span_len, key_start
        )
        lse_block = lax.dynamic_slice_in_dim(log_sums, block_index * block_len, block_len, 1)
        prob_full = jnp.exp(scores - lse_block[:, :, None])
        prob_low = prob_full.astype(jnp.bfloat16)
        grad_block = lax.dynamic_slice_in_dim(grad_att, block_index * block_len, block_len, 0)
        grad_prob = jnp.einsum(
            "qhd,khd->hqk", grad_block, v_block, preferred_element_type=jnp.float32
        )
        delta_row = jnp.sum(prob_full * grad_prob, axis=-1, keepdims=True)
        grad_score = (prob_full * (grad_prob - delta_row)).astype(jnp.bfloat16)
        grad_q = (
            jnp.einsum("hqk,khd->qhd", grad_score, k_block, preferred_element_type=jnp.float32)
            * scale
        )
        grad_k = (
            jnp.einsum("hqk,qhd->khd", grad_score, q_block, preferred_element_type=jnp.float32)
            * scale
        )
        grad_v = jnp.einsum(
            "hqk,qhd->khd", prob_low, grad_block, preferred_element_type=jnp.float32
        )
        return (grad_q, grad_k, grad_v)

    def padded_short(block_index, own_start, wide_start):
        grad_q, grad_k, grad_v = span_backward(block_index, short_len, own_start)
        zero_pad = jnp.zeros((2 * short_len, head_count, head_dim), jnp.float32)
        offset = own_start - wide_start
        return (
            grad_q,
            lax.dynamic_update_slice_in_dim(zero_pad, grad_k, offset, 0),
            lax.dynamic_update_slice_in_dim(zero_pad, grad_v, offset, 0),
        )

    def block_step(block_index, carried):
        grad_query, grad_keys, grad_values = carried
        slot_index = block_index // per_slot
        own_start = slot_index * short_len
        wide_start = jnp.maximum(slot_index - 1, 0) * short_len
        grad_q, grad_k, grad_v = lax.cond(
            seg_start[slot_index] == 1,
            lambda: padded_short(block_index, own_start, wide_start),
            lambda: span_backward(block_index, 2 * short_len, wide_start),
        )
        grad_query = lax.dynamic_update_slice_in_dim(grad_query, grad_q, block_index * block_len, 0)
        grad_keys = grad_keys + grad_k
        grad_values = grad_values + grad_v
        return (grad_query, grad_keys, grad_values)

    zero_state = jnp.zeros((row_count, head_count, head_dim), jnp.float32)
    return lax.fori_loop(
        0, row_count // block_len, block_step, (zero_state, zero_state, zero_state)
    )


def per_device(layer_in, value_first, seg_start, gain_one, w_qkv, w_out, gain_two, w_mlp, grad_out):
    share_rows, model_width = layer_in.shape
    share_width = w_qkv.shape[1]
    head_count = share_width // HEAD_DIM
    tok_start = lax.axis_index("narrow") * share_rows
    gathered = gather_rows(layer_in)
    row_count = gathered.shape[0]
    short_len = row_count // seg_start.shape[0]
    shaped = (row_count, head_count, HEAD_DIM)
    seg_tok = jnp.repeat(jnp.cumsum(seg_start), short_len)
    positions = (
        ((1 - seg_start)[:, None] * short_len + jnp.arange(short_len, dtype=jnp.int32)[None, :])
        .reshape(row_count)
        .astype(jnp.float32)
    )
    cosine, sine_vals = rope_tables(positions)
    inputs_f = gathered.astype(jnp.float32)
    inverse_one_full = lax.rsqrt(jnp.mean(inputs_f * inputs_f, axis=-1, keepdims=True) + EPSILON)
    normed = (inputs_f * inverse_one_full * gain_one).astype(jnp.bfloat16)
    inverse_one = lax.dynamic_slice_in_dim(inverse_one_full, tok_start, share_rows, 0)
    query_raw = contract_cols(normed, w_qkv[0])
    key_raw = contract_cols(normed, w_qkv[1])
    own_values = contract_cols(normed, w_qkv[2])
    query_vals = rotate(query_raw.reshape(shaped), cosine, sine_vals).astype(jnp.bfloat16)
    key_vals = rotate(key_raw.reshape(shaped), cosine, sine_vals).astype(jnp.bfloat16)
    first_heads = lax.all_to_all(value_first, "narrow", split_axis=1, concat_axis=0, tiled=True)
    mixed_vals = (
        (0.5 * own_values + 0.5 * first_heads.astype(jnp.float32))
        .astype(jnp.bfloat16)
        .reshape(shaped)
    )
    attended, log_sums = attend_forward(
        query_vals, key_vals, mixed_vals, seg_start, seg_tok, short_len
    )
    attended_low = attended.reshape(row_count, share_width).astype(jnp.bfloat16)
    share_in = layer_in.astype(jnp.float32)
    attn_share = head_sum(product(attended_low, w_out))
    hidden_share = share_in + attn_share
    hidden_full = gather_full(hidden_share)
    inverse_full = lax.rsqrt(jnp.mean(hidden_full * hidden_full, axis=-1, keepdims=True) + EPSILON)
    normed_two = (hidden_full * inverse_full * gain_two).astype(jnp.bfloat16)
    inverse_two = lax.dynamic_slice_in_dim(inverse_full, tok_start, share_rows, 0)
    weights_all = lax.all_gather(w_mlp, "wide", axis=0, tiled=True)
    w_gate = weights_all[:, 0, :]
    w_up = weights_all[:, 1, :]
    w_down = weights_all[:, 2, :]
    gate_vals = product(normed_two, w_gate)
    up_vals = product(normed_two, w_up)
    sigmoid_gate = jax.nn.sigmoid(gate_vals)
    silu_gate = gate_vals * sigmoid_gate
    inner_act = (silu_gate * up_vals).astype(jnp.bfloat16)
    mlp_share = narrow_sum(contract_cols(inner_act, w_down))
    layer_out = (hidden_share + mlp_share).astype(jnp.bfloat16)
    grad_rows = gather_rows(grad_out)
    grad_inner = product(grad_rows, w_down)
    grad_gate = (
        grad_inner * up_vals * sigmoid_gate * (1.0 + gate_vals * (1.0 - sigmoid_gate))
    ).astype(jnp.bfloat16)
    grad_up = (grad_inner * silu_gate).astype(jnp.bfloat16)
    grad_normed_two = contract_cols(grad_gate, w_gate) + contract_cols(grad_up, w_up)
    grad_w_mlp = lax.psum_scatter(
        jnp.stack(
            [
                contract_rows(normed_two, grad_gate),
                contract_rows(normed_two, grad_up),
                contract_rows(grad_rows, inner_act),
            ],
            axis=1,
        ),
        "wide",
        scatter_dimension=0,
        tiled=True,
    )
    grad_two_share = narrow_sum(grad_normed_two)
    grad_two_full = gather_full(grad_two_share)
    scaled = grad_two_full * gain_two
    dot_two = jnp.sum(scaled * hidden_full, axis=-1, keepdims=True)
    grad_hidden_full = (
        grad_rows.astype(jnp.float32)
        + scaled * inverse_full
        - hidden_full * inverse_full**3 * dot_two / model_width
    )
    grad_hidden = lax.dynamic_slice_in_dim(grad_hidden_full, tok_start, share_rows, 0)
    grad_attn = grad_hidden_full.astype(jnp.bfloat16)
    grad_gain_two = jnp.sum(grad_two_share * hidden_share * inverse_two, axis=0)
    grad_w_out = contract_rows(attended_low, grad_attn)
    grad_att = contract_cols(grad_attn, w_out).astype(jnp.bfloat16).reshape(shaped)
    grad_query, grad_keys, grad_mixed = attend_backward(
        query_vals, key_vals, mixed_vals, grad_att, log_sums, seg_start, seg_tok, short_len
    )
    grad_q_low = (
        rotate(grad_query, cosine, -sine_vals).reshape(row_count, share_width).astype(jnp.bfloat16)
    )
    grad_k_low = (
        rotate(grad_keys, cosine, -sine_vals).reshape(row_count, share_width).astype(jnp.bfloat16)
    )
    grad_mix_low = lax.optimization_barrier(
        grad_mixed.reshape(row_count, share_width).astype(jnp.bfloat16)
    )
    grad_own = (0.5 * grad_mix_low.astype(jnp.float32)).astype(jnp.bfloat16)
    grad_w_qkv = jnp.stack(
        [
            contract_rows(grad_q_low, normed),
            contract_rows(grad_k_low, normed),
            contract_rows(grad_own, normed),
        ]
    )
    grad_value_first = lax.all_to_all(
        grad_own, "narrow", split_axis=0, concat_axis=1, tiled=True
    ).astype(jnp.float32)
    grad_normed = (
        product(grad_q_low, w_qkv[0]) + product(grad_k_low, w_qkv[1]) + product(grad_own, w_qkv[2])
    )
    grad_one_share = head_sum(grad_normed)
    dot_one = jnp.sum(grad_one_share * gain_one * share_in, axis=-1, keepdims=True)
    grad_in = (
        grad_hidden
        + grad_one_share * gain_one * inverse_one
        - share_in * inverse_one**3 * dot_one / model_width
    )
    grad_gain_one = jnp.sum(grad_one_share * share_in * inverse_one, axis=0)
    grad_w_qkv, grad_w_out = lax.psum((grad_w_qkv, grad_w_out), "wide")
    first_f = value_first.astype(jnp.float32)
    value_sums, grad_gain_one, grad_gain_two = lax.psum(
        (
            jnp.stack([jnp.sum(first_f * first_f), jnp.sum(own_values * own_values)]),
            grad_gain_one,
            grad_gain_two,
        ),
        ("wide", "narrow"),
    )
    entries = share_rows * model_width * lax.axis_size("wide") * lax.axis_size("narrow")
    value_norms = jnp.sqrt(value_sums / entries)
    return (
        layer_out,
        grad_in,
        grad_value_first,
        grad_gain_one,
        grad_w_qkv,
        grad_w_out,
        grad_gain_two,
        grad_w_mlp,
        value_norms,
    )


def solution(mesh):
    placed = (
        P(("wide", "narrow"), None),
        P(("wide", "narrow"), None),
        P("wide"),
        P(),
        P(None, "narrow", None),
        P("narrow", None),
        P(),
        P("wide", None, "narrow"),
        P(("wide", "narrow"), None),
    )
    return jax.shard_map(
        per_device,
        mesh=mesh,
        in_specs=placed,
        out_specs=(
            P(("wide", "narrow"), None),
            P(("wide", "narrow"), None),
            P(("wide", "narrow"), None),
            P(),
            P(None, "narrow", None),
            P("narrow", None),
            P(),
            P("wide", None, "narrow"),
            P(),
        ),
        check_vma=False,
    )
```

profile of v0, /device:TPU:0, one launch (start us, length us, event | category | flops | bytes accessed | tf_op | source)
XLA Modules:
  0.0 1476.3 jit_solution(3869161934671717775)
XLA Ops:
  10.2 6.3 all-to-all-start
  19.8 50.9 %all-to-all-done = bf16[512,4,256]{0,2,1:T(8,128)(2,1)} async-done(((bf16[512,4,256]{0,2,1:T(8,128)(2,1)}), bf16[512,4,256]{0,2,1:T(8,128)(2,1)}, u32[]{:S(2)}, u32[]{:S(2)}) %all-to-all-start) | async-done | bytes 1048608 | tf_op jit(solution)/shard_map/all_to_all | solution.py:212
  73.8 36.6 %all-gather.6.cloned.1.call-done = bf16[2048,1024]{1,0:T(8,128)(2,1)} async-done(((bf16[512,1024]{1,0:T(8,128)(2,1)}), bf16[2048,1024]{1,0:T(8,128)(2,1)}) %all-gather.6.cloned.1.call-update) | async-done | bytes 4194320 | tf_op jit(solution)/shard_map/all_gather | solution.py:51
  123.2 43.6 %while.40 = (s32[]{:T(128)}, bf16[2048,4,64]{0,2,1:T(8,128)(2,1)S(1)}, f32[4,2048]{1,0:T(4,128)S(1)}, s32[2]{0:T(128)S(1)}, bf16[2048,4,64]{0,2,1:T(8,128)(2,1)}...) while((s32[]{:T(128)}, ...), condition=%wide.region_9.10_spmd.clone, body=%wide.region_2.9_spmd.clone.sunk | while | flops 1127219712 | bytes 57813548 | solution.py:119
  125.0 9.4 conditional.6
  135.8 9.4 conditional.6
  146.6 9.4 conditional.6
  157.4 9.4 conditional.6
  171.5 155.8 %reduce-scatter.6.cloned.1.call-done = f32[512,1024]{1,0:T(8,128)} async-done(((f32[2048,1024]{1,0:T(8,128)}), f32[512,1024]{1,0:T(8,128)}) %reduce-scatter.6.cloned.1.call-update) | async-done | bytes 2097168 | tf_op jit(solution)/shard_map/reduce_scatter | solution.py:59
  331.9 149.2 %all-gather.8.cloned.1.call-done = f32[2048,1024]{1,0:T(8,128)} async-done(((f32[512,1024]{1,0:T(8,128)}), f32[2048,1024]{1,0:T(8,128)}) %all-gather.8.cloned.1.call-update) | async-done | bytes 8388624 | tf_op jit(solution)/shard_map/all_gather | solution.py:63
  489.5 29.5 %all-gather.10.cloned.1.call-done = bf16[1024,3,704]{0,2,1:T(8,128)(2,1)} async-done(((bf16[128,3,704]{0,2,1:T(8,128)(2,1)}), bf16[1024,3,704]{0,2,1:T(8,128)(2,1)}) %all-gather.10.cloned.1.call-update) | async-done | bytes 4325392 | tf_op jit(solution)/shard_map/all_gather | solution.py:229
  519.0 8.4 fusion.90
  527.3 6.6 fusion.89
  534.0 67.2 %all-gather.12.cloned.1.call-done = bf16[2048,1024]{1,0:T(8,128)(2,1)} async-done(((bf16[512,1024]{1,0:T(8,128)(2,1)}), bf16[2048,1024]{1,0:T(8,128)(2,1)}) %all-gather.12.cloned.1.call-update) | async-done | bytes 4194320 | tf_op jit(solution)/shard_map/all_gather | solution.py:51
  601.2 11.1 multiply_convert_fusion.3
  612.2 5.9 fusion.88
  618.2 7.3 convolution_add_fusion
  625.5 143.2 %reduce-scatter.10.cloned.1.call-done = f32[512,1024]{1,0:T(8,128)} async-done(((f32[2048,1024]{1,0:T(8,128)}), f32[512,1024]{1,0:T(8,128)}) %reduce-scatter.10.cloned.1.call-update) | async-done | bytes 2097168 | tf_op jit(solution)/shard_map/reduce_scatter | solution.py:55
  769.2 9.1 fusion.92
  778.4 142.2 %all-gather.14.cloned.1.call-done = f32[2048,1024]{1,0:T(8,128)} async-done(((f32[512,1024]{1,0:T(8,128)}), f32[2048,1024]{1,0:T(8,128)}) %all-gather.14.cloned.1.call-update) | async-done | bytes 8388624 | tf_op jit(solution)/shard_map/all_gather | solution.py:63
  920.6 6.8 multiply_reduce_fusion.2
  929.5 5.9 multiply_subtract_fusion
  940.6 167.4 %while.41 = (s32[]{:T(128)}, f32[2048,4,64]{0,2,1:T(8,128)}, f32[2048,4,64]{0,2,1:T(8,128)}, f32[2048,4,64]{0,2,1:T(8,128)}, s32[2]{0:T(128)S(1)}, /*index=5*/bf...) while((s32[]{:T(128)}, f32[2048,4,64]{0,2,1:T(8,128)}, ...), condition=%wide.region_20.21_spmd.clone, body=%wide.region_15.20_spmd.clone.sunk | while | flops 2753167872 | bytes 190434032 | solution.py:182
  942.2 33.8 %conditional.7 = (f32[512,4,64]{0,2,1:T(8,128)S(1)}, f32[2048,4,64]{0,2,1:T(8,128)}, f32[2048,4,64]{0,2,1:T(8,128)}) conditional(s32[]{:T(128)} %bitcast.150, (s32[]{:T(128)}, s32[]{:T(128)}, s32[2048]{0:T(1024)S(1)}, bf16[2048,4,64]{0,2,1:T(8,128)(2,1)}, bf16[2048,4,64]{0,2,1:T(8,128)(2,1)}, /*index=5*/f32[4,2048]{1,0:T(4,128)S(1)}, ...), branch_computations={%region_16.17_spmd, %region_18.19_spmd} | conditional | flops 2751070720 | bytes 176777376 | solution.py:171
  950.2 5.7 dynamic_update_slice.37
  956.0 5.9 multiply_reduce_fusion.1
  970.2 5.7 dynamic_update_slice.36
  976.8 5.5 select_add_fusion.3
  983.7 34.1 %conditional.7 = (f32[512,4,64]{0,2,1:T(8,128)S(1)}, f32[2048,4,64]{0,2,1:T(8,128)}, f32[2048,4,64]{0,2,1:T(8,128)}) conditional(s32[]{:T(128)} %bitcast.150, (s32[]{:T(128)}, s32[]{:T(128)}, s32[2048]{0:T(1024)S(1)}, bf16[2048,4,64]{0,2,1:T(8,128)(2,1)}, bf16[2048,4,64]{0,2,1:T(8,128)(2,1)}, /*index=5*/f32[4,2048]{1,0:T(4,128)S(1)}, ...), branch_computations={%region_16.17_spmd, %region_18.19_spmd} | conditional | flops 2751070720 | bytes 176777376 | solution.py:171
  991.7 5.8 dynamic_update_slice.37
  997.5 6.2 multiply_reduce_fusion.1
  1012.0 5.7 dynamic_update_slice.36
  1018.6 6.7 select_add_fusion.3
  1026.7 32.3 %conditional.7 = (f32[512,4,64]{0,2,1:T(8,128)S(1)}, f32[2048,4,64]{0,2,1:T(8,128)}, f32[2048,4,64]{0,2,1:T(8,128)}) conditional(s32[]{:T(128)} %bitcast.150, (s32[]{:T(128)}, s32[]{:T(128)}, s32[2048]{0:T(1024)S(1)}, bf16[2048,4,64]{0,2,1:T(8,128)(2,1)}, bf16[2048,4,64]{0,2,1:T(8,128)(2,1)}, /*index=5*/f32[4,2048]{1,0:T(4,128)S(1)}, ...), branch_computations={%region_16.17_spmd, %region_18.19_spmd} | conditional | flops 2751070720 | bytes 176777376 | solution.py:171
  1034.7 5.0 dynamic_update_slice.37
  1039.7 6.0 multiply_reduce_fusion.1
  1054.0 5.0 dynamic_update_slice.36
  1059.9 6.7 select_add_fusion.3
  1068.0 32.2 %conditional.7 = (f32[512,4,64]{0,2,1:T(8,128)S(1)}, f32[2048,4,64]{0,2,1:T(8,128)}, f32[2048,4,64]{0,2,1:T(8,128)}) conditional(s32[]{:T(128)} %bitcast.150, (s32[]{:T(128)}, s32[]{:T(128)}, s32[2048]{0:T(1024)S(1)}, bf16[2048,4,64]{0,2,1:T(8,128)(2,1)}, bf16[2048,4,64]{0,2,1:T(8,128)(2,1)}, /*index=5*/f32[4,2048]{1,0:T(4,128)S(1)}, ...), branch_computations={%region_16.17_spmd, %region_18.19_spmd} | conditional | flops 2751070720 | bytes 176777376 | solution.py:171
  1081.0 5.9 multiply_reduce_fusion.1
  1101.0 6.6 select_add_fusion.3
  1120.2 5.9 convolution_bitcast_fusion
  1147.2 6.3 fusion.85
  1165.8 30.2 %all-to-all-done.1 = bf16[4,512,256]{1,2,0:T(8,128)(2,1)} async-done(((bf16[4,512,256]{1,2,0:T(8,128)(2,1)}), bf16[4,512,256]{1,2,0:T(8,128)(2,1)}, u32[]{:S(2)}, u32[]{:S(2)}) %all-to-all-start.1) | async-done | bytes 1048608 | tf_op jit(solution)/shard_map/all_to_all | solution.py:294
  1201.8 95.8 %reduce-scatter.12.cloned.1.call-done = f32[512,1024]{1,0:T(8,128)} async-done(((f32[2048,1024]{1,0:T(8,128)}), f32[512,1024]{1,0:T(8,128)}) %reduce-scatter.12.cloned.1.call-update) | async-done | bytes 2097168 | tf_op jit(solution)/shard_map/reduce_scatter | solution.py:59
  1299.9 46.3 %all-reduce = (f32[1024]{0:T(1024)}, f32[1024]{0:T(1024)}, f32[2]{0:T(128)S(1)}) all-reduce(f32[1024]{0:T(1024)S(1)} %get-tuple-element.709, f32[1024]{0:T(1024)S(1)} %get-tuple-element.777, f32[2]{0:T(128)S(1)} %pad_maximum_fusion.4), channel_id=1, replica_groups=mesh['wide'=8,'narrow'=4] {'wide','narrow'}, use_global_device_ids=true, to_apply=%region_24.25 | all-reduce | flops 2050 | bytes 16400 | tf_op jit(solution)/shard_map/psum | solution.py:310
  1351.2 28.6 %reduce-scatter.14.cloned.1.call-done = f32[128,3,704]{0,2,1:T(8,128)} async-done(((f32[1024,3,704]{0,2,1:T(8,128)}), f32[128,3,704]{0,2,1:T(8,128)}) %reduce-scatter.14.cloned.1.call-update) | async-done | bytes 1081360 | tf_op jit(solution)/shard_map/reduce_scatter | solution.py:247
  1379.8 84.8 %all-reduce.4.cloned.1.call-done = (f32[3,256,1024]{2,1,0:T(8,128)}, f32[256,1024]{1,0:T(8,128)}) async-done(((f32[3,256,1024]{2,1,0:T(8,128)}, f32[256,1024]{1,0:T(8,128)}), (f32[3,256,1024]{2,1,0:T(8,128)}, f32[256,1024]{1,0:T(8,128)})) %all-reduce.4.cloned.1.call-update) | async-done | bytes 4194320 | tf_op jit(solution)/shard_map/psum | solution.py:308
  (308 shorter events, 232.4 us)
Async XLA Ops:
  7.2 159.7 %copy-start = (bf16[256,1024]{1,0:T(8,128)(2,1)S(1)}, bf16[256,1024]{1,0:T(8,128)(2,1)}, u32[]{:S(2)}) copy-start(bf16[256,1024]{1,0:T(8,128)(2,1)} %param.22) | copy-start | bytes 1572868
  7.2 9.4 copy-start.38
  7.2 9.8 copy-start.19
  7.2 103.1 %all-gather.6.cloned.1.call-start = ((), (), s32[]{:S(2)}) async-start(), calls=%async_computation.7 | async-start | bytes 5242880 | tf_op jit(solution)/shard_map/all_gather | solution.py:51
  10.2 60.5 %all-to-all-start = ((bf16[512,4,256]{0,2,1:T(8,128)(2,1)}), bf16[512,4,256]{0,2,1:T(8,128)(2,1)}, u32[]{:S(2)}, u32[]{:S(2)}) async-start(bf16[512,4,256]{0,2,1:T(8,128)(2,1)} %bitcast.12), calls=%async_computation | async-start | bytes 2097152 | tf_op jit(solution)/shard_map/all_to_all | solution.py:212
  16.6 310.8 %reduce-scatter.6.cloned.1.call-start = ((), (), s32[]{:S(2)}) async-start(), calls=%async_computation.8 | async-start | bytes 10485760 | tf_op jit(solution)/shard_map/reduce_scatter | solution.py:59
  19.8 101.2 %copy-start.26 = (f32[2048,32]{0,1:T(8,128)}, f32[2048,32]{0,1:T(8,128)S(1)}, u32[]{:S(2)}) copy-start(f32[2048,32]{0,1:T(8,128)S(1)} %get-tuple-element.787) | copy-start | bytes 786436
  72.2 41.4 %copy-start.36 = (f32[1024]{0:T(1024)S(1)}, f32[1024]{0:T(1024)}, u32[]{:S(2)}) copy-start(f32[1024]{0:T(1024)} %param.20) | copy-start | bytes 12292
  110.4 3.4 copy-start.14
  114.9 4.8 copy-start.23
  166.9 4.6 copy-start.15
  171.4 155.9 %copy-start.12 = (bf16[512,1024]{1,0:T(8,128)(2,1)S(1)}, bf16[512,1024]{1,0:T(8,128)(2,1)}, u32[]{:S(2)}) copy-start(bf16[512,1024]{1,0:T(8,128)(2,1)} %param.17) | copy-start | bytes 3145732
  171.5 309.6 %all-gather.8.cloned.1.call-start = ((), (), s32[]{:S(2)}) async-start(), calls=%async_computation.9 | async-start | bytes 10485760 | tf_op jit(solution)/shard_map/all_gather | solution.py:63
  330.7 188.3 %all-gather.10.cloned.1.call-start = ((), (), s32[]{:S(2)}) async-start(), calls=%async_computation.10 | async-start | bytes 4866048 | tf_op jit(solution)/shard_map/all_gather | solution.py:229
  331.3 269.9 %all-gather.12.cloned.1.call-start = ((), (), s32[]{:S(2)}) async-start(), calls=%async_computation.12 | async-start | bytes 5242880 | tf_op jit(solution)/shard_map/all_gather | solution.py:51
  331.9 153.4 %copy-start.35 = (f32[1024]{0:T(1024)S(1)}, f32[1024]{0:T(1024)}, u32[]{:S(2)}) copy-start(f32[1024]{0:T(1024)} %param.23) | copy-start | bytes 12292
  331.9 436.9 %reduce-scatter.10.cloned.1.call-start = ((), (), s32[]{:S(2)}) async-start(), calls=%async_computation.13 | async-start | bytes 10485760 | tf_op jit(solution)/shard_map/reduce_scatter | solution.py:55
  481.1 5.8 copy-start.7
  485.3 442.1 %copy-start.33 = (f32[2048]{0:T(1024)}, f32[2048]{0:T(1024)S(1)}, u32[]{:S(2)}) copy-start(f32[2048]{0:T(1024)S(1)} %get-tuple-element.789) | copy-start | bytes 24580
  519.0 8.4 copy-start.21
  612.2 6.0 copy-start.41
  612.2 6.0 copy-start.39
  625.5 295.1 %all-gather.14.cloned.1.call-start = ((), (), s32[]{:S(2)}) async-start(), calls=%async_computation.14 | async-start | bytes 10485760 | tf_op jit(solution)/shard_map/all_gather | solution.py:63
  768.8 393.5 %reduce-scatter.8.cloned.1.call-start = ((), (), s32[]{:S(2)}) async-start(), calls=%async_computation.11 | async-start | bytes 10485760 | tf_op jit(solution)/shard_map/reduce_scatter | solution.py:55
  778.3 519.3 %reduce-scatter.12.cloned.1.call-start = ((), (), s32[]{:S(2)}) async-start(), calls=%async_computation.15 | async-start | bytes 10485760 | tf_op jit(solution)/shard_map/reduce_scatter | solution.py:59
  920.6 8.9 copy-start.9
  935.4 3.6 copy-start.6
  940.6 169.4 %copy-start.27 = (f32[2048,32]{0,1:T(8,128)S(1)}, f32[2048,32]{0,1:T(8,128)}, u32[]{:S(2)}) copy-start(f32[2048,32]{0,1:T(8,128)} %copy-done.26) | copy-start | bytes 786436
  945.3 3.3 copy-start.3
  956.0 6.0 copy-start.4
  986.8 3.3 copy-start.3
  997.5 6.3 copy-start.4
  1029.8 3.3 copy-start.3
  1039.7 6.1 copy-start.4
  1071.1 3.3 copy-start.3
  1081.0 6.0 copy-start.4
  1120.2 259.6 %reduce-scatter.14.cloned.1.call-start = ((), (), s32[]{:S(2)}) async-start(), calls=%async_computation.16 | async-start | bytes 9732096 | tf_op jit(solution)/shard_map/reduce_scatter | solution.py:247
  1120.2 6.0 copy-start.22
  1120.2 6.0 copy-start.42
  1137.7 58.3 %all-to-all-start.1 = ((bf16[4,512,256]{1,2,0:T(8,128)(2,1)}), bf16[4,512,256]{1,2,0:T(8,128)(2,1)}, u32[]{:S(2)}, u32[]{:S(2)}) async-start(bf16[4,512,256]{1,2,0:T(8,128)(2,1)} %bitcast.163), calls=%async_computation.5 | async-start | bytes 2097152 | tf_op jit(solution)/shard_map/all_to_all | solution.py:294
  1141.9 322.6 %all-reduce.4.cloned.1.call-start = ((), (), s32[]{:S(2)}) async-start(), calls=%async_computation.17 | async-start | bytes 8388608 | tf_op jit(solution)/shard_map/psum | solution.py:308
  1142.2 3.6 copy-start.18
  1142.2 3.8 copy-start.24
  1156.8 5.4 copy-start.11
  1165.8 131.8 %copy-start.13 = (bf16[512,1024]{1,0:T(8,128)(2,1)S(1)}, bf16[512,1024]{1,0:T(8,128)(2,1)}, u32[]{:S(2)}) copy-start(bf16[512,1024]{1,0:T(8,128)(2,1)} %param.17) | copy-start | bytes 3145732
  1165.8 131.8 %copy-start.37 = (f32[1024]{0:T(1024)S(1)}, f32[1024]{0:T(1024)}, u32[]{:S(2)}) copy-start(f32[1024]{0:T(1024)} %param.20) | copy-start | bytes 12292
  1464.6 4.1 copy-start.29
  1464.6 5.1 copy-start.1
  (15 other events, 32.3 us)
Sparse Core Ops, SparseCore 0:
  9.6 100.7 all-gather.5
  171.6 155.6 reduce-scatter.5
  330.8 150.2 all-gather.7
  482.8 36.0 all-gather.9
  520.4 80.7 all-gather.11
  625.6 143.0 reduce-scatter.9
  770.3 150.2 all-gather.13
  922.9 142.7 reduce-scatter.7
  1120.3 177.2 reduce-scatter.11
  1301.5 78.2 reduce-scatter.13
  1383.7 80.8 all-reduce.3
where the time goes:
time: 1490 us; the launch traced here: 1480 us
  waiting for transfers between devices  1020 us (68%)
  matrix products  179 us (12%)
  other arithmetic  109 us (7%)
  local copies, waits for them, and re-layouts  92.6 us (6%)
  blocking collectives  46.3 us (3%)
    all_gather x2, waiting for transfers between devices, gather_full(): return lax.all_gather(values, 'narrow', axis=0, tiled=True)  291 us
    reduce_scatter x2, waiting for transfers between devices, head_sum(): return lax.psum_scatter(values, 'narrow', scatter_dimension=0, tiled=True)  252 us
    reduce_scatter x2, waiting for transfers between devices, narrow_sum(): return lax.psum_scatter(values, 'narrow', scatter_dimension=0, tiled=True)  143 us
    all_gather x2, waiting for transfers between devices, gather_rows(): return lax.all_gather(values, 'narrow', axis=0, tiled=True)  104 us
    psum x1, waiting for transfers between devices, per_device(): grad_w_qkv, grad_w_out = lax.psum((grad_w_qkv, grad_w_out), 'wide')  84.8 us
    all_to_all x1, waiting for transfers between devices, per_device(): lax.all_to_all(value_first, 'narrow', split_axis=1, concat_axis=0, tiled=...  50.9 us
    psum x1, blocking collectives, per_device(): lax.psum((jnp.stack([jnp.sum(first_f * first_f), jnp.sum(own_values * own...  46.3 us
    dot_general x7, matrix products, product(): return jnp.dot(left_side, right_side, preferred_element_type=jnp.float32)  37.9 us
  transfers between devices with their start and end apart: 13, of which 12 were waited for; matrix products, arithmetic and copies ran while one was open for 19% of the time, Pallas kernels for 0%

commit v1 on v0

v1 whole, which is shorter than its diff:
```python
import functools

import jax
import jax.numpy as jnp
from jax import lax
from jax.experimental import pallas as pl
from jax.experimental.pallas import tpu as pltpu
from jax.sharding import Mesh, PartitionSpec as P

HEAD_DIM = 64
EPSILON = 1e-06
BF = jnp.bfloat16
F32 = jnp.float32
AXES = ("hi", "core", "zh", "zq")
MESH = pl.DeviceIdType.MESH
ANY = pl.BlockSpec(memory_space=pl.ANY)
VM = pl.BlockSpec(memory_space=pltpu.VMEM)
VMEM_MAX = 62 << 20
DMA = pltpu.SemaphoreType.DMA


def nn(a, b):
    return lax.dot_general(a, b, (((1,), (0,)), ((), ())), preferred_element_type=F32)


def nt(a, b):
    return lax.dot_general(a, b, (((1,), (1,)), ((), ())), preferred_element_type=F32)


def tn(a, b):
    return lax.dot_general(a, b, (((0,), (0,)), ((), ())), preferred_element_type=F32)


def coords():
    return tuple(lax.axis_index(name) for name in AXES)


def remote(src, dst, send, recv, to):
    return pltpu.make_async_remote_copy(
        src_ref=src, dst_ref=dst, send_sem=send, recv_sem=recv, device_id=to, device_id_type=MESH
    )


def greet_plane(sizes, with_hi):
    hi_n, _, _, nh = sizes
    h, c, r, q = coords()
    barrier = pltpu.get_barrier_semaphore()
    count = 0
    for dc in range(2):
        for dr in range(2):
            for dq in range(nh):
                if dc or dr or dq:
                    to = (h, (c + dc) % 2, (r + dr) % 2, (q + dq) % nh)
                    pl.semaphore_signal(barrier, inc=1, device_id=to, device_id_type=MESH)
                    count += 1
    if with_hi:
        for dh in range(1, hi_n):
            to = ((h + dh) % hi_n, c, r, q)
            pl.semaphore_signal(barrier, inc=1, device_id=to, device_id_type=MESH)
            count += 1
    pl.semaphore_wait(barrier, count)


def rotate_lanes(values, first):
    width = values.shape[1]
    if width < 128:
        return jnp.concatenate([values[:, 32:], values[:, :32]], axis=1)
    return jnp.where(
        first, pltpu.roll(values, width - 32, 1), pltpu.roll(values, 32, 1)
    )


def first_lanes(rows, width):
    lane = lax.broadcasted_iota(jnp.int32, (rows, width), 1)
    return lane % HEAD_DIM < HEAD_DIM // 2


def lane_window(pair, pw, sw):
    return slice(0, sw) if pw == sw else pl.ds(pl.multiple_of(pair * pw, pw), pw)


def tiled(table, width):
    times = width // table.shape[1]
    return table if times == 1 else jnp.concatenate([table] * times, axis=1)


def exchange_kernel(
    sizes, chunks, x, v, w, sg, xa, va, ws, so, xs, wb, sb, vb,
    swap_s, swap_r, peer_s, peer_r, core_s, core_r, w_s, w_r, wh_s, wh_r, sg_s, sg_r, v_s, v_r, loc,
):
    hi_n, _, _, nh = sizes
    n = 2 * nh
    h, c, r, q = coords()
    p = c * nh + q
    partner_p = r * nh + q
    rows = x.shape[0] // chunks
    same = c == r
    other = c != r
    partner = (h, r, c, q)
    mate = (h, 1 - c, r, q)
    greet_plane(sizes, True)

    def part(k):
        return pl.ds(k * rows, rows)

    def swap_x(k):
        return remote(x.at[part(k)], xa.at[partner_p, part(k)], swap_s.at[k], swap_r.at[k], partner)

    def own_arrives(k):
        return remote(x.at[part(k)], xa.at[p, part(k)], swap_s.at[k], swap_r.at[k], partner)

    def push_peer(src, k, dq):
        to = (h, c, r, (q + dq) % nh)
        return remote(src, xa.at[p, part(k)], peer_s.at[dq, k], peer_r.at[dq, k], to)

    def push_mate(src, k, dq):
        block = c * nh + (q + nh - dq) % nh
        return remote(src, xa.at[block, part(k)], core_s.at[dq, k], core_r.at[dq, k], mate)

    def send_w():
        return remote(w.at[h], ws.at[h], w_s, w_r, partner)

    def spread_w(dh):
        to = ((h + dh) % hi_n, c, r, q)
        return remote(ws.at[h], ws.at[h], wh_s.at[dh], wh_r.at[dh], to)

    def send_sg():
        return remote(sg, so, sg_s, sg_r, partner)

    local_x_in = pltpu.make_async_copy(x, xs, loc.at[0])
    local_w_in = pltpu.make_async_copy(w, wb, loc.at[1])
    local_s_in = pltpu.make_async_copy(sg, sb, loc.at[2])
    local_v_in = pltpu.make_async_copy(v.at[p], vb, loc.at[3])
    local_x_out = pltpu.make_async_copy(xs, xa.at[p], loc.at[4])
    local_w_out = pltpu.make_async_copy(wb, ws, loc.at[5])
    local_s_out = pltpu.make_async_copy(sb, so, loc.at[6])
    local_v_out = pltpu.make_async_copy(vb, va.at[p], loc.at[7])

    @pl.when(other)
    def _():
        send_sg().start()
        send_w().start()
        for k in range(chunks):
            swap_x(k).start()

    @pl.when(same)
    def _():
        for k in range(chunks):
            for dq in range(1, nh):
                push_peer(x.at[part(k)], k, dq).start()
            push_mate(x.at[part(k)], k, 0).start()
        local_x_in.start()
        local_w_in.start()
        local_s_in.start()
        local_v_in.start()

    @pl.when(other)
    def _():
        for k in range(chunks):
            own_arrives(k).wait_recv()
            for dq in range(1, nh):
                push_peer(xa.at[p, part(k)], k, dq).start()
            push_mate(xa.at[p, part(k)], k, 0).start()
        send_w().wait_recv()
        for dh in range(1, hi_n):
            spread_w(dh).start()

    @pl.when(same)
    def _():
        local_x_in.wait()
        local_x_out.start()
        local_w_in.wait()
        local_w_out.start()
        local_s_in.wait()
        local_s_out.start()
        local_v_in.wait()
        local_v_out.start()

    def send_v(s):
        to = (h, s // nh, c, s % nh)
        return remote(v.at[s], va.at[r * nh + q], v_s.at[s], v_r.at[r * nh + q], to)

    for s in range(n):
        @pl.when(jnp.logical_or(other, p != s))
        def _():
            send_v(s).start()

    for k in range(chunks):
        for dq in range(1, nh):
            block = c * nh + (q + nh - dq) % nh
            remote(
                x.at[part(k)], xa.at[block, part(k)], peer_s.at[dq, k], peer_r.at[dq, k], mate
            ).wait_recv()
            push_mate(xa.at[block, part(k)], k, dq).start()

    for k in range(chunks):
        for dq in range(nh):
            block = (1 - c) * nh + (q + nh - dq) % nh
            remote(
                x.at[part(k)], xa.at[block, part(k)], core_s.at[dq, k], core_r.at[dq, k], mate
            ).wait_recv()

    @pl.when(other)
    def _():
        send_sg().wait_recv()
        for dh in range(1, hi_n):
            source = (h + hi_n - dh) % hi_n
            remote(ws.at[source], ws.at[source], wh_s.at[dh], wh_r.at[dh], mate).wait_recv()
        send_sg().wait_send()
        send_w().wait_send()
        for dh in range(1, hi_n):
            spread_w(dh).wait_send()
        for k in range(chunks):
            swap_x(k).wait_send()

    for b in range(n):
        @pl.when(jnp.logical_or(other, p != b))
        def _():
            remote(v.at[0], va.at[b], v_s.at[b], v_r.at[b], mate).wait_recv()

    for s in range(n):
        @pl.when(jnp.logical_or(other, p != s))
        def _():
            send_v(s).wait_send()

    for k in range(chunks):
        for dq in range(1, nh):
            push_peer(x.at[part(k)], k, dq).wait_send()
        for dq in range(nh):
            push_mate(x.at[part(k)], k, dq).wait_send()

    @pl.when(same)
    def _():
        local_x_out.wait()
        local_w_out.wait()
        local_s_out.wait()
        local_v_out.wait()


def exchange_inputs(sizes, x, v, w, sg):
    hi_n, _, _, nh = sizes
    n = 2 * nh
    tok, width = x.shape
    sw = v.shape[2]
    chunks = 4 if tok % 64 == 0 else 1
    return pl.pallas_call(
        functools.partial(exchange_kernel, sizes, chunks),
        out_shape=(
            jax.ShapeDtypeStruct((n, tok, width), BF),
            jax.ShapeDtypeStruct((n, tok, sw), BF),
            jax.ShapeDtypeStruct(w.shape, BF),
            jax.ShapeDtypeStruct(sg.shape, F32),
        ),
        in_specs=[ANY] * 4,
        out_specs=(ANY,) * 4,
        scratch_shapes=[
            pltpu.VMEM((tok, width), BF),
            pltpu.VMEM(w.shape, BF),
            pltpu.VMEM(sg.shape, F32),
            pltpu.VMEM((tok, sw), BF),
            DMA((chunks,)), DMA((chunks,)),
            DMA((nh, chunks)), DMA((nh, chunks)),
            DMA((nh, chunks)), DMA((nh, chunks)),
            DMA, DMA,
            DMA((hi_n,)), DMA((hi_n,)),
            DMA, DMA,
            DMA((n,)), DMA((n,)),
            DMA((8,)),
        ],
        name="exchange_inputs",
        compiler_params=pltpu.CompilerParams(collective_id=1, has_side_effects=True),
        cost_estimate=pl.CostEstimate(flops=0, bytes_accessed=160 << 20, transcendentals=0),
    )(x, v, w, sg)


def masked(scores, diagonal, crossing, causal, bias):
    if diagonal:
        return jnp.where(causal, scores, -1e30)
    if crossing:
        return scores + bias
    return scores


def forward_kernel(
    sizes, block, xa, ws, va, g1, cos, sin, bias_ref,
    ai, qo, ko, mo, ao, lse, own, att_s, att_r, loc,
):
    _, _, _, nh = sizes
    n = 2 * nh
    h, c, r, q = coords()
    p = c * nh + q
    row_len, sw = va.shape
    tok = row_len // n
    short = row_len // 2
    pw = cos.shape[1]
    pairs = sw // pw
    halves = pw // HEAD_DIM
    greet_plane(sizes, False)
    br = 256
    own[...] = jnp.zeros_like(own)

    def project(i, carry):
        rows = pl.ds(pl.multiple_of(i * br, br), br)
        xf = xa[rows, :].astype(F32)
        inv = lax.rsqrt(jnp.mean(xf * xf, axis=-1, keepdims=True) + EPSILON)
        normed = (xf * inv * g1[...]).astype(BF)
        raw = nt(normed, ws[...])
        first = first_lanes(br, sw)
        ct = tiled(cos[rows, :], sw)
        st = tiled(sin[rows, :], sw)
        q_raw = raw[:, :sw]
        k_raw = raw[:, sw : 2 * sw]
        own_vals = raw[:, 2 * sw :]
        q_rot = (q_raw * ct + rotate_lanes(q_raw, first) * st).astype(BF)
        qo[rows, :] = (q_rot.astype(F32) * HEAD_DIM**-0.5).astype(BF)
        ko[rows, :] = (k_raw * ct + rotate_lanes(k_raw, first) * st).astype(BF)
        mo[rows, :] = (0.5 * own_vals + 0.5 * va[rows, :].astype(F32)).astype(BF)
        own[...] += jnp.sum((own_vals * own_vals).reshape(br // 8, 8, sw), axis=0)
        return carry

    lax.fori_loop(0, row_len // br, project, 0)

    bias = bias_ref[0:1, 0:1]
    blocks = row_len // block
    per = block // tok
    causal = lax.broadcasted_iota(jnp.int32, (block, block), 0) >= lax.broadcasted_iota(
        jnp.int32, (block, block), 1
    )

    def send(b, pair):
        lanes = lane_window(pair, pw, sw)
        to = (h, b // nh, r, b % nh)
        return remote(
            ao.at[b, :, lanes], ai.at[p, :, lanes], att_s.at[pair, b], att_r.at[pair, p], to
        )

    def keep(pair):
        lanes = lane_window(pair, pw, sw)
        return pltpu.make_async_copy(ao.at[p, :, lanes], ai.at[p, :, lanes], loc.at[pair])

    def pair_step(pair, carry):
        lanes = lane_window(pair, pw, sw)
        for i in range(blocks):
            outs = []
            rows = pl.ds(i * block, block)
            for half in range(halves):
                cols = slice(half * HEAD_DIM, (half + 1) * HEAD_DIM)
                qh = qo[rows, lanes][:, cols]
                score = []
                for j in range(i + 1):
                    kj = ko[pl.ds(j * block, block), lanes][:, cols]
                    crossing = i * block >= short and j * block < short
                    score.append(masked(nt(qh, kj), i == j, crossing, causal, bias))
                top = functools.reduce(
                    jnp.maximum, [jnp.max(s, axis=-1, keepdims=True) for s in score]
                )
                total = 0.0
                acc = 0.0
                for j in range(i + 1):
                    e = jnp.exp(score[j] - top)
                    total = total + jnp.sum(e, axis=-1, keepdims=True)
                    vj = mo[pl.ds(j * block, block), lanes][:, cols]
                    acc = acc + nn(e.astype(BF), vj)
                outs.append(acc / total)
                lse[pair, rows, half : half + 1] = top + jnp.log(total)
            out = (jnp.concatenate(outs, axis=1) if halves > 1 else outs[0]).astype(BF)
            for t in range(per):
                b = i * per + t
                ao[b, :, lanes] = out[t * tok : (t + 1) * tok]

                @pl.when(p != b)
                def _():
                    send(b, pair).start()

        keep(pair).start()
        return carry

    lax.fori_loop(0, pairs, pair_step, 0)

    def drain(pair, carry):
        lanes = lane_window(pair, pw, sw)
        for b in range(n):
            @pl.when(p != b)
            def _():
                send(b, pair).wait_send()
                remote(
                    ao.at[b, :, lanes], ai.at[b, :, lanes], att_s.at[pair, b], att_r.at[pair, b],
                    (h, 1 - c, r, q),
                ).wait_recv()
        keep(pair).wait()
        return carry

    lax.fori_loop(0, pairs, drain, 0)


def attention_forward(sizes, xa, ws, va, g1, cos, sin, bias):
    _, _, _, nh = sizes
    n = 2 * nh
    row_len, sw = va.shape
    tok = row_len // n
    pw = cos.shape[1]
    pairs = sw // pw
    block = max(tok, 512)
    flops = 2 * row_len * xa.shape[1] * 3 * sw + 2 * row_len * row_len * sw
    return pl.pallas_call(
        functools.partial(forward_kernel, sizes, block),
        out_shape=(
            jax.ShapeDtypeStruct((n, tok, sw), BF),
            jax.ShapeDtypeStruct((row_len, sw), BF),
            jax.ShapeDtypeStruct((row_len, sw), BF),
            jax.ShapeDtypeStruct((row_len, sw), BF),
            jax.ShapeDtypeStruct((n, tok, sw), BF),
            jax.ShapeDtypeStruct((pairs, row_len, pw // HEAD_DIM), F32),
            jax.ShapeDtypeStruct((8, sw), F32),
        ),
        in_specs=[VM] * 7,
        out_specs=(ANY,) + (VM,) * 6,
        scratch_shapes=[DMA((pairs, n)), DMA((pairs, n)), DMA((pairs,))],
        name="attention_forward",
        compiler_params=pltpu.CompilerParams(
            collective_id=2, has_side_effects=True, vmem_limit_bytes=VMEM_MAX
        ),
        cost_estimate=pl.CostEstimate(
            flops=4 * flops, bytes_accessed=16 << 20, transcendentals=row_len * row_len * sw // 128
        ),
    )(xa, ws, va, g1, cos, sin, bias)


def mlp_kernel(
    p_ref, x, ai, dy, g2, wo, wm, lo, gh, ga, dwm, dwo, gg2, hid, n2, acc_o, acc_g
):
    step = pl.program_id(0)
    n = ai.shape[0]
    wide = wm.shape[0]
    width = x.shape[2]
    dw = width // wide

    @pl.when(step == 0)
    def _():
        total = x[0].astype(F32)
        for s in range(n):
            total = total + nn(ai[s], wo[s])
        hid[...] = total
        inv = lax.rsqrt(jnp.mean(total * total, axis=-1, keepdims=True) + EPSILON)
        n2[...] = (total * inv * g2[...]).astype(BF)
        acc_o[...] = jnp.zeros_like(acc_o)
        acc_g[...] = jnp.zeros_like(acc_g)

    def weight(j):
        return jnp.concatenate([wm[w, 0, j] for w in range(wide)], axis=1)

    def put(j, grad):
        low = grad.astype(BF)
        for w in range(wide):
            dwm[w, 0, j] = low[:, w * dw : (w + 1) * dw]

    gate = nt(n2[...], weight(0))
    up = nt(n2[...], weight(1))
    sig = jax.nn.sigmoid(gate)
    silu = gate * sig
    inner = (silu * up).astype(BF)
    grad_inner = nt(dy[...], weight(2))
    grad_gate = (grad_inner * up * sig * (1.0 + gate * (1.0 - sig))).astype(BF)
    grad_up = (grad_inner * silu).astype(BF)
    acc_o[...] += nn(inner, weight(2))
    acc_g[...] += nn(grad_gate, weight(0)) + nn(grad_up, weight(1))
    put(0, tn(grad_gate, n2[...]))
    put(1, tn(grad_up, n2[...]))
    put(2, tn(inner, dy[...]))

    @pl.when(step == pl.num_programs(0) - 1)
    def _():
        hidden = hid[...]
        lo[...] = (hidden + acc_o[...]).astype(BF)
        inv = lax.rsqrt(jnp.mean(hidden * hidden, axis=-1, keepdims=True) + EPSILON)
        grad_n = acc_g[...]
        gg2[...] = jnp.sum((grad_n * hidden * inv).reshape(-1, 8, width), axis=0)
        scaled = grad_n * g2[...]
        dot = jnp.sum(scaled * hidden, axis=-1, keepdims=True)
        grad_h = dy[...].astype(F32) + scaled * inv - hidden * (inv * inv * inv * dot / width)
        gh[...] = grad_h
        low = grad_h.astype(BF)
        for s in range(n):
            ga[s] = nt(low, wo[s]).astype(BF)
            dwo[s] = tn(ai[s], low).astype(BF)


def feed_forward(place, xa, ai, dy, g2, wo, wm):
    n, tok, sw = ai.shape
    width = dy.shape[1]
    wide, _, _, ffs, dw = wm.shape

    def whole(*shape):
        return pl.BlockSpec(shape, lambda i, p: (0,) * len(shape))

    chunk = pl.BlockSpec((wide, 1, 3, ffs, dw), lambda i, p: (0, i, 0, 0, 0))
    return pl.pallas_call(
        mlp_kernel,
        out_shape=(
            jax.ShapeDtypeStruct((tok, width), BF),
            jax.ShapeDtypeStruct((tok, width), F32),
            jax.ShapeDtypeStruct((n, tok, sw), BF),
            jax.ShapeDtypeStruct(wm.shape, BF),
            jax.ShapeDtypeStruct((n, sw, width), BF),
            jax.ShapeDtypeStruct((8, width), F32),
        ),
        grid_spec=pltpu.PrefetchScalarGridSpec(
            num_scalar_prefetch=1,
            grid=(n,),
            in_specs=[
                pl.BlockSpec((1, tok, width), lambda i, p: (p[0], 0, 0)),
                whole(n, tok, sw),
                whole(tok, width),
                whole(1, width),
                whole(n, sw, width),
                chunk,
            ],
            out_specs=(
                whole(tok, width),
                whole(tok, width),
                whole(n, tok, sw),
                chunk,
                whole(n, sw, width),
                whole(8, width),
            ),
            scratch_shapes=[
                pltpu.VMEM((tok, width), F32),
                pltpu.VMEM((tok, width), BF),
                pltpu.VMEM((tok, width), F32),
                pltpu.VMEM((tok, width), F32),
            ],
        ),
        name="feed_forward",
        compiler_params=pltpu.CompilerParams(
            dimension_semantics=("arbitrary",), vmem_limit_bytes=VMEM_MAX
        ),
        cost_estimate=pl.CostEstimate(
            flops=18 * tok * width * ffs * n, bytes_accessed=40 << 20, transcendentals=tok * ffs * n
        ),
    )(place, xa, ai, dy, g2, wo, wm)


def backward_kernel(
    sizes, block, ga, xa, ws, g1, cos, sin, bias_ref, qi, ki, mi, ao, lse, gh,
    gv, gi, dwq, gg1,
    do, normed, dq, dk, dv, dcat, gow, gnp, rcv, rcv2, gis,
    do_s, do_r, gv_s, gv_r, co_s, co_r, pe_s, pe_r, gi_s, gi_r, loc,
):
    _, _, _, nh = sizes
    n = 2 * nh
    h, c, r, q = coords()
    p = c * nh + q
    row_len, sw = qi.shape
    width = xa.shape[1]
    tok = row_len // n
    short = row_len // 2
    pw = cos.shape[1]
    pairs = sw // pw
    halves = pw // HEAD_DIM
    same = c == r
    mate = (h, 1 - c, r, q)
    greet_plane(sizes, False)

    def send_do(s):
        to = (h, s // nh, r, s % nh)
        return remote(ga.at[s], do.at[p], do_s.at[s], do_r.at[p], to)

    keep_do = pltpu.make_async_copy(ga.at[p], do.at[p], loc.at[0])
    for s in range(n):
        @pl.when(p != s)
        def _():
            send_do(s).start()

    keep_do.start()
    br = 256

    def norm(i, carry):
        rows = pl.ds(pl.multiple_of(i * br, br), br)
        xf = xa[rows, :].astype(F32)
        inv = lax.rsqrt(jnp.mean(xf * xf, axis=-1, keepdims=True) + EPSILON)
        normed[rows, :] = (xf * inv * g1[...]).astype(BF)
        return carry

    lax.fori_loop(0, row_len // br, norm, 0)
    keep_do.wait()
    for s in range(n):
        @pl.when(p != s)
        def _():
            remote(ga.at[s], do.at[s], do_s.at[s], do_r.at[s], mate).wait_recv()
            send_do(s).wait_send()

    bias = bias_ref[0:1, 0:1]
    blocks = row_len // block
    per = block // tok
    causal = lax.broadcasted_iota(jnp.int32, (block, block), 0) >= lax.broadcasted_iota(
        jnp.int32, (block, block), 1
    )

    def send_gv(b, pair):
        lanes = lane_window(pair, pw, sw)
        to = (h, r, b // nh, b % nh)
        return remote(
            gow.at[b, :, lanes], gv.at[p, :, lanes], gv_s.at[pair, b], gv_r.at[pair, p], to
        )

    def keep_gv(pair):
        lanes = lane_window(pair, pw, sw)
        return pltpu.make_async_copy(gow.at[p, :, lanes], gv.at[p, :, lanes], loc.at[1 + pair])

    def pair_step(pair, carry):
        lanes = lane_window(pair, pw, sw)
        dk[...] = jnp.zeros_like(dk)
        dv[...] = jnp.zeros_like(dv)
        for i in range(blocks):
            rows = pl.ds(i * block, block)
            pieces = [[] for _ in range(i + 1)]
            dq_parts = []
            do_rows = [do[i * per + t, :, lanes] for t in range(per)]
            do_i = do_rows[0] if per == 1 else jnp.concatenate(do_rows, axis=0)
            ao_rows = [ao[i * per + t, :, lanes] for t in range(per)]
            ao_i = ao_rows[0] if per == 1 else jnp.concatenate(ao_rows, axis=0)
            product = do_i.astype(F32) * ao_i.astype(F32)
            for half in range(halves):
                cols = slice(half * HEAD_DIM, (half + 1) * HEAD_DIM)
                qh = qi[rows, lanes][:, cols]
                doh = do_i[:, cols]
                delta = jnp.sum(product[:, cols], axis=-1, keepdims=True)
                level = lse[pair, rows, half : half + 1]
                acc = 0.0
                for j in range(i + 1):
                    kj = ki[pl.ds(j * block, block), lanes][:, cols]
                    vj = mi[pl.ds(j * block, block), lanes][:, cols]
                    crossing = i * block >= short and j * block < short
                    score = masked(nt(qh, kj), i == j, crossing, causal, bias)
                    prob = jnp.exp(score - level)
                    grad_prob = nt(doh, vj)
                    grad_score = (prob * (grad_prob - delta)).astype(BF)
                    acc = acc + nn(grad_score, kj)
                    pieces[j].append((tn(grad_score, qh), tn(prob.astype(BF), doh)))
                dq_parts.append(acc * HEAD_DIM**-0.5)
            dq[rows, :] = dq_parts[0] if halves == 1 else jnp.concatenate(dq_parts, axis=1)
            for j in range(i + 1):
                at = pl.ds(j * block, block)
                if halves == 1:
                    dk[at, :] += pieces[j][0][0]
                    dv[at, :] += pieces[j][0][1]
                else:
                    dk[at, :] += jnp.concatenate([t[0] for t in pieces[j]], axis=1)
                    dv[at, :] += jnp.concatenate([t[1] for t in pieces[j]], axis=1)
        first = first_lanes(br, pw)

        def finish(i, inner_carry):
            rows = pl.ds(pl.multiple_of(i * br, br), br)
            ct = cos[rows, :]
            st = sin[rows, :]
            a = dq[rows, :]
            b = dk[rows, :]
            dcat[0, rows, lanes] = (a * ct - rotate_lanes(a, first) * st).astype(BF)
            dcat[1, rows, lanes] = (b * ct - rotate_lanes(b, first) * st).astype(BF)
            dcat[2, rows, lanes] = (0.5 * dv[rows, :].astype(BF).astype(F32)).astype(BF)
            return inner_carry

        lax.fori_loop(0, row_len // br, finish, 0)
        for b in range(n):
            gow[b, :, lanes] = dcat[2, pl.ds(b * tok, tok), lanes]

            @pl.when(jnp.logical_or(c != r, p != b))
            def _():
                send_gv(b, pair).start()

        @pl.when(same)
        def _():
            keep_gv(pair).start()

        return carry

    lax.fori_loop(0, pairs, pair_step, 0)

    ck = min(256, tok)
    half_rows = row_len // 2
    n_half = half_rows // ck
    n_blk = tok // ck

    def partial(base, k):
        rows = pl.ds(pl.multiple_of(base + k * ck, ck), ck)
        total = nn(dcat[0, rows, :], ws[:sw, :])
        for t in range(1, 3):
            total = total + nn(dcat[t, rows, :], ws[t * sw : (t + 1) * sw, :])
        gnp[rows, :] = total.astype(BF)

    def to_mate(k):
        rows = pl.ds(pl.multiple_of((1 - c) * half_rows + k * ck, ck), ck)
        return remote(gnp.at[rows], rcv.at[pl.ds(k * ck, ck)], co_s.at[k], co_r.at[k], mate)

    for k in range(n_half):
        partial((1 - c) * half_rows, k)
        to_mate(k).start()

    def own_rows(d):
        return ((q + d) % nh) * tok

    def to_peer(d, k):
        rows = pl.ds(pl.multiple_of(c * half_rows + own_rows(d) + k * ck, ck), ck)
        to = (h, c, r, (q + d) % nh)
        return remote(
            gnp.at[rows], rcv2.at[d - 1, pl.ds(k * ck, ck)], pe_s.at[d, k], pe_r.at[d, k], to
        )

    for d in range(1, nh + 1):
        for k in range(n_blk):
            partial(c * half_rows + own_rows(d), k)

    for k in range(n_half):
        to_mate(k).wait_recv()

    def added(d, k):
        rows = pl.ds(pl.multiple_of(c * half_rows + own_rows(d) + k * ck, ck), ck)
        theirs = pl.ds(pl.multiple_of(own_rows(d) + k * ck, ck), ck)
        return rows, gnp[rows, :].astype(F32) + rcv[theirs, :].astype(F32)

    for d in range(1, nh):
        for k in range(n_blk):
            rows, total = added(d, k)
            gnp[rows, :] = total.astype(BF)
            to_peer(d, k).start()

    for t in range(3):
        dwq[t * sw : (t + 1) * sw, :] = tn(dcat[t], normed[...]).astype(BF)

    partner = (h, r, c, q)
    gg1[...] = jnp.zeros_like(gg1)

    def send_gi(k):
        rows = pl.ds(k * ck, ck)
        return remote(gis.at[rows], gi.at[rows], gi_s.at[k], gi_r.at[k], partner)

    def keep_gi(k):
        rows = pl.ds(k * ck, ck)
        return pltpu.make_async_copy(gis.at[rows], gi.at[rows], gi_s.at[k])

    for k in range(n_blk):
        for d in range(1, nh):
            to_peer(d, k).wait_recv()
        _, grad_n = added(0, k)
        for d in range(1, nh):
            grad_n = grad_n + rcv2[d - 1, pl.ds(k * ck, ck), :].astype(F32)
        here = pl.ds(pl.multiple_of(p * tok + k * ck, ck), ck)
        xf = xa[here, :].astype(F32)
        inv = lax.rsqrt(jnp.mean(xf * xf, axis=-1, keepdims=True) + EPSILON)
        gg1[...] += jnp.sum((grad_n * xf * inv).reshape(-1, 8, width), axis=0)
        scaled = grad_n * g1[...]
        dot = jnp.sum(scaled * xf, axis=-1, keepdims=True)
        rows = pl.ds(k * ck, ck)
        gis[rows, :] = (
            gh[rows, :] + scaled * inv - xf * (inv * inv * inv * dot / width)
        ).astype(BF)

        @pl.when(c != r)
        def _():
            send_gi(k).start()

        @pl.when(same)
        def _():
            keep_gi(k).start()

    for k in range(n_blk):
        @pl.when(c != r)
        def _():
            send_gi(k).wait_send()
            send_gi(k).wait_recv()

        @pl.when(same)
        def _():
            keep_gi(k).wait()

    for k in range(n_half):
        to_mate(k).wait_send()
    for d in range(1, nh):
        for k in range(n_blk):
            to_peer(d, k).wait_send()

    def drain(pair, carry):
        lanes = lane_window(pair, pw, sw)
        for b in range(n):
            @pl.when(jnp.logical_or(c != r, p != b))
            def _():
                send_gv(b, pair).wait_send()
                remote(
                    gow.at[b, :, lanes], gv.at[b, :, lanes], gv_s.at[pair, b], gv_r.at[pair, b], mate
                ).wait_recv()

        @pl.when(same)
        def _():
            keep_gv(pair).wait()

        return carry

    lax.fori_loop(0, pairs, drain, 0)


def attention_backward(sizes, ga, xa, ws, g1, cos, sin, bias, qi, ki, mi, ao, lse, gh):
    _, _, _, nh = sizes
    n, tok, sw = ga.shape
    row_len, width = xa.shape
    pw = cos.shape[1]
    pairs = sw // pw
    block = max(tok, 512)
    ck = min(256, tok)
    n_half = row_len // 2 // ck
    n_blk = tok // ck
    return pl.pallas_call(
        functools.partial(backward_kernel, sizes, block),
        out_shape=(
            jax.ShapeDtypeStruct((n, tok, sw), BF),
            jax.ShapeDtypeStruct((tok, width), BF),
            jax.ShapeDtypeStruct((3 * sw, width), BF),
            jax.ShapeDtypeStruct((8, width), F32),
        ),
        in_specs=[ANY] + [VM] * 12,
        out_specs=(ANY, ANY, VM, VM),
        scratch_shapes=[
            pltpu.VMEM((n, tok, sw), BF),
            pltpu.VMEM((row_len, width), BF),
            pltpu.VMEM((row_len, pw), F32),
            pltpu.VMEM((row_len, pw), F32),
            pltpu.VMEM((row_len, pw), F32),
            pltpu.VMEM((3, row_len, sw), BF),
            pltpu.VMEM((n, tok, sw), BF),
            pltpu.VMEM((row_len, width), BF),
            pltpu.VMEM((row_len // 2, width), BF),
            pltpu.VMEM((max(nh - 1, 1), tok, width), BF),
            pltpu.VMEM((tok, width), BF),
            DMA((n,)), DMA((n,)),
            DMA((pairs, n)), DMA((pairs, n)),
            DMA((n_half,)), DMA((n_half,)),
            DMA((nh, n_blk)), DMA((nh, n_blk)),
            DMA((n_blk,)), DMA((n_blk,)),
            DMA((1 + pairs,)),
        ],
        name="attention_backward",
        compiler_params=pltpu.CompilerParams(
            collective_id=3, has_side_effects=True, vmem_limit_bytes=VMEM_MAX
        ),
        cost_estimate=pl.CostEstimate(
            flops=60 << 30, bytes_accessed=24 << 20, transcendentals=row_len * row_len * sw // 128
        ),
    )(ga, xa, ws, g1, cos, sin, bias, qi, ki, mi, ao, lse, gh)


def per_device(sizes, layer_in, value_first, seg_start, gain_one, w_qkv, w_out, gain_two, w_mlp, grad_out):
    hi_n, _, _, nh = sizes
    n = 2 * nh
    wide = 2 * hi_n
    tok, width = layer_in.shape
    sw = w_qkv.shape[1]
    ffs = w_mlp.shape[2]
    dw = w_mlp.shape[0]
    row_len = n * tok
    short = row_len // seg_start.shape[0]
    h, c, r, q = coords()
    place = (c * nh + q).astype(jnp.int32)

    w_mlp_t = jnp.transpose(w_mlp, (1, 2, 0)).reshape(3 * ffs, dw)
    wm = lax.all_gather(w_mlp_t, AXES, axis=0, tiled=False).reshape(wide, n, 3, ffs, dw)
    wo = lax.all_gather(w_out, ("zh", "zq"), axis=0, tiled=False)

    swap = [
        (((a * 2 + b) * 2 + d) * nh + e, ((a * 2 + d) * 2 + b) * nh + e)
        for a in range(hi_n)
        for b in range(2)
        for d in range(2)
        for e in range(nh)
    ]
    v_cut = value_first.reshape(tok, n, sw).transpose(1, 0, 2)
    sg = jnp.full((8, 128), seg_start[1].astype(F32))
    w_cut = w_qkv.reshape(hi_n, 3 * sw // hi_n, width)
    xa, va, ws, so = exchange_inputs(sizes, layer_in, v_cut, w_cut, sg)
    ws = ws.reshape(3 * sw, width)
    dy = lax.ppermute(grad_out, AXES, swap)

    joined = 1.0 - so[0, 0]
    index = jnp.arange(row_len, dtype=jnp.int32)
    slot = index // short
    positions = (index - slot * short).astype(F32) + jnp.where(slot == 1, joined * short, 0.0)
    pw = min(sw, 128)
    half_dim = HEAD_DIM // 2
    frequency = 10000.0 ** (-2.0 * jnp.arange(half_dim, dtype=F32) / HEAD_DIM)
    angles = positions[:, None] * frequency[None, :]
    cosine, sine = jnp.cos(angles), jnp.sin(angles)
    times = pw // HEAD_DIM
    cos = jnp.concatenate([cosine, cosine] * times, axis=1)
    sin = jnp.concatenate([-sine, sine] * times, axis=1)
    bias = (1.0 - joined) * jnp.full((8, 128), -1e30, F32)

    g1 = gain_one.reshape(1, width)
    g2 = gain_two.reshape(1, width)
    xr = xa.reshape(row_len, width)
    ai, qo, ko, mo, ao, lse, own = attention_forward(
        sizes, xr, ws, va.reshape(row_len, sw), g1, cos, sin, bias
    )
    lo, gh, ga, dwm, dwo, gg2 = feed_forward(place.reshape(1), xa, ai, dy, g2, wo, wm)
    layer_out = lax.ppermute(lo, AXES, swap)

    dwm = lax.psum_scatter(dwm, ("hi", "core"), scatter_dimension=0, tiled=True)
    dwm = lax.psum_scatter(dwm, ("zh", "zq"), scatter_dimension=1, tiled=True)
    grad_w_mlp = jnp.transpose(dwm.reshape(3, ffs, dw).astype(F32), (2, 0, 1))
    dwo = lax.psum_scatter(dwo, ("zh", "zq"), scatter_dimension=0, tiled=True)
    grad_w_out = lax.psum(dwo.reshape(sw, width), ("hi", "core")).astype(F32)

    gv, gi, dwq, gg1 = attention_backward(
        sizes, ga, xr, ws, g1, cos, sin, bias, qo, ko, mo, ao, lse, gh
    )
    grad_value_first = gv.transpose(1, 0, 2).reshape(tok, width).astype(F32)
    grad_in = gi.astype(F32)

    dwq = lax.psum_scatter(dwq, ("hi", "zh"), scatter_dimension=0, tiled=True)
    dwq = lax.all_gather(dwq, ("core", "hi", "zh"), axis=0, tiled=False)
    dwq = dwq.reshape(2, 3 * sw, width)
    grad_w_qkv = lax.dynamic_index_in_dim(dwq, r, 0, keepdims=False)
    grad_w_qkv = grad_w_qkv.reshape(3, sw, width).astype(F32)

    first_f = value_first.astype(F32)
    sums = jnp.concatenate(
        [
            jnp.sum(gg1, axis=0),
            jnp.sum(gg2, axis=0),
            jnp.sum(first_f * first_f).reshape(1),
            jnp.sum(own).reshape(1),
        ]
    )
    sums = lax.psum(sums, AXES)
    entries = tok * width * wide * n
    value_norms = jnp.sqrt(sums[2 * width :] / entries)
    return (
        layer_out,
        grad_in,
        grad_value_first,
        sums[:width],
        grad_w_qkv,
        grad_w_out,
        sums[width : 2 * width],
        grad_w_mlp,
        value_norms,
    )


def solution(mesh):
    wide, narrow = mesh.shape["wide"], mesh.shape["narrow"]
    sizes = (wide // 2, 2, 2, narrow // 2)
    fine = Mesh(mesh.devices.reshape(sizes), AXES)
    w_axes, n_axes = ("hi", "core"), ("zh", "zq")
    rows = P(AXES, None)
    return jax.shard_map(
        functools.partial(per_device, sizes),
        mesh=fine,
        in_specs=(
            rows,
            rows,
            P(w_axes),
            P(),
            P(None, n_axes, None),
            P(n_axes, None),
            P(),
            P(w_axes, None, n_axes),
            rows,
        ),
        out_specs=(
            rows,
            rows,
            rows,
            P(),
            P(None, n_axes, None),
            P(n_axes, None),
            P(),
            P(w_axes, None, n_axes),
            P(),
        ),
        check_vma=False,
    )
```

time: 1490 us -> 750 us (0.50)
  waiting for transfers between devices: 1020 us -> 313 us
  Pallas kernels: 0 us -> 329 us
  matrix products: 179 us -> 0 us
  other arithmetic: 109 us -> 17.1 us
  local copies, waits for them, and re-layouts: 92.6 us -> 16.9 us
    all_gather x5 -> x3, waiting for transfers between devices: 425 us -> 85.4 us  [the longest x1 46 us: per_device(): dwq = lax.all_gather(dwq, ('core', 'hi', 'zh'), axis=0, tiled=False)]
    pallas_call x0 -> x4, Pallas kernels: none -> 329 us  [the longest x1 121 us: attention_backward(): pl.pallas_call(functools.partial(backward_kernel, sizes, block), out_shap...]
    reduce_scatter x5 -> x4, waiting for transfers between devices: 423 us -> 225 us  [the longest x1 121 us: per_device(): dwm = lax.psum_scatter(dwm, ('hi', 'core'), scatter_dimension=0, tiled=True)]
    dot_general x49 -> x0, matrix products: 179 us -> none  [the longest x7 37.9 us: product(): return jnp.dot(left_side, right_side, preferred_element_type=jnp.float32)]
    psum x1, waiting for transfers between devices: 84.8 us -> 0.01 us  [per_device(): grad_w_out = lax.psum(dwo.reshape(sw, width), ('hi', 'core')).astype(F32)]
    all_to_all x2 -> x0, waiting for transfers between devices: 81.1 us -> none  [the longest x1 50.9 us: per_device(): lax.all_to_all(value_first, 'narrow', split_axis=1, concat_axis=0, tiled=...]
    dynamic_update_slice x20 -> x0, local copies, waits for them, and re-layouts: 46.4 us -> none  [the longest x4 21.5 us: padded_short(): lax.dynamic_update_slice_in_dim(zero_pad, grad_v, offset, 0)]
    reduce_sum x10 -> x4, other arithmetic: 31.9 us -> 1.77 us  [the longest x1 1.14 us: per_device(): jnp.sum(first_f * first_f).reshape(1)]
  transfers between devices with their start and end apart: 13 -> 10, of which waited for: 12 -> 5; matrix products, arithmetic and copies ran while one was open for 19% -> 4% of each run, Pallas kernels for 0% -> 38%
where the time goes in v1:
time: 750 us; the launch traced here: 743 us
  Pallas kernels  329 us (44%)
  waiting for transfers between devices  313 us (42%)
  blocking collectives  39.3 us (5%)
  other arithmetic  17.1 us (2%)
  local copies, waits for them, and re-layouts  16.9 us (2%)
  between operations  15.9 us (2%)
  starting transfers between devices  11.7 us (2%)
    reduce_scatter x1, waiting for transfers between devices, per_device(): dwm = lax.psum_scatter(dwm, ('hi', 'core'), scatter_dimension=0, tiled=True)  121 us
    pallas_call x1, Pallas kernels, attention_backward(): pl.pallas_call(functools.partial(backward_kernel, sizes, block), out_shap...  121 us
    pallas_call x1, Pallas kernels, exchange_inputs(): pl.pallas_call(functools.partial(exchange_kernel, sizes, chunks), out_sha...  118 us
    reduce_scatter x1, waiting for transfers between devices, per_device(): dwq = lax.psum_scatter(dwq, ('hi', 'zh'), scatter_dimension=0, tiled=True)  61.9 us
    pallas_call x1, Pallas kernels, attention_forward(): pl.pallas_call(functools.partial(forward_kernel, sizes, block), out_shape...  46.6 us
    all_gather x1, waiting for transfers between devices, per_device(): dwq = lax.all_gather(dwq, ('core', 'hi', 'zh'), axis=0, tiled=False)  46 us
    pallas_call x1, Pallas kernels, feed_forward(): pl.pallas_call(mlp_kernel, out_shape=(jax.ShapeDtypeStruct((tok, width),...  43.3 us
    reduce_scatter x1, waiting for transfers between devices, per_device(): dwm = lax.psum_scatter(dwm, ('zh', 'zq'), scatter_dimension=1, tiled=True)  42.4 us
  transfers between devices with their start and end apart: 10, of which 5 were waited for; matrix products, arithmetic and copies ran while one was open for 4% of the time, Pallas kernels for 38%

profile of v1, /device:TPU:0, one launch (start us, length us, event | category | flops | bytes accessed | tf_op | source)
XLA Modules:
  0.0 743.3 jit_solution(16952860258355915836)
XLA Ops:
  7.2 0.0 all-gather.8.cloned.1.call-start
  7.2 0.7 all-gather.8.cloned.1.call-update
  7.9 0.0 all-gather.6.cloned.1.call-start
  8.0 0.7 all-gather.6.cloned.1.call-update
  8.7 0.0 reduce-scatter.7.cloned.1.call-start
  8.7 1.9 collective-permute-start
  10.6 1.2 slice.15
  12.5 1.5 copy.26
  14.0 1.3 copy.27
  15.3 0.6 broadcast_in_dim.14.sg
  15.9 118.5 %exchange_inputs.1 = (bf16[4,512,1024]{2,1,0:T(8,128)(2,1)}, bf16[4,512,256]{2,1,0:T(8,128)(2,1)}, bf16[4,192,1024]{2,1,0:T(8,128)(2,1)}, f32[8,128]{1,0:T(8,128)}) custom-call(bf16[512,1024]{1,0:T(8,128)(2,1)} %x.1, bf16[4,512,256]{2,1,0:T(8,128)(2,1)} %bitcast.34, bf16[4,192,1024]{2,1,0:T(8,128)(2,1)} %bitcast.35, f32[8,128]{1,0:T(8,128)} %broadcast_in_dim.14.sg), custom_call_target="tpu_custom_call" | custom-call | bytes 167772160 | tf_op jit(solution)/shard_map/exchange_inputs/pallas_call | solution.py:246
  134.4 1.2 slice.16
  136.3 3.7 fusion
  140.0 3.0 pad_maximum_fusion
  143.0 0.6 mul.53.bias_ref
  143.6 46.6 %attention_forward.1 = (bf16[4,512,256]{2,1,0:T(8,128)(2,1)}, bf16[2048,256]{1,0:T(8,128)(2,1)}, bf16[2048,256]{1,0:T(8,128)(2,1)}, bf16[2048,256]{1,0:T(8,128)(...) custom-call(bf16[2048,1024]{1,0:T(8,128)(2,1)} %bitcast.40, ...), custom_call_target="tpu_custom_call" | custom-call | flops 21474836480 | bytes 16777216 | tf_op jit(solution)/shard_map/attention_forward/pallas_call | solution.py:405
  190.3 0.0 all-gather.8.cloned.1.call-done
  190.3 39.4 %all-gather.6.cloned.1.call-done = bf16[32,2112,128]{2,1,0:T(8,128)(2,1)} async-done(((bf16[1,2112,128]{2,1,0:T(8,128)(2,1)}), bf16[32,2112,128]{2,1,0:T(8,128)(2,1)}) %all-gather.6.cloned.1.call-update) | async-done | bytes 17301520 | tf_op jit(solution)/shard_map/all_gather | solution.py:864
  229.7 43.3 %feed_forward.1 = (bf16[512,1024]{1,0:T(8,128)(2,1)}, f32[512,1024]{1,0:T(8,128)}, bf16[4,512,256]{2,1,0:T(8,128)(2,1)}, bf16[8,4,3,704,128]{4,3,2,1,0:T(8,128)(...) custom-call(s32[1]{0:T(128)} %bitcast.p_ref, bf16[4,512,1024]{2,1,0:T(8,128)(2,1)} %get-tuple-element.30.x, ...), custom_call_target="tpu_custom_call" | custom-call | flops 26575110144 | bytes 41943040 | tf_op jit(solution)/shard_map/feed_forward/pallas_call | solution.py:497
  272.9 0.0 reduce-scatter.7.cloned.1.call-update
  272.9 0.0 reduce-scatter.5.cloned.1.call-start
  273.0 120.9 %attention_backward.1 = (bf16[4,512,256]{2,1,0:T(8,128)(2,1)}, bf16[512,1024]{1,0:T(8,128)(2,1)}, bf16[768,1024]{1,0:T(8,128)(2,1)}, f32[8,1024]{1,0:T(8,128)}) custom-call(bf16[4,512,256]{2,1,0:T(8,128)(2,1)} %get-tuple-element.36.ga, bf16[2048,1024]{1,0:T(8,128)(2,1)} %bitcast.41, bf16[768,1024]{1,0:T(8,128)(2,1)} %bitcast.44, f32[1,1024]{1,0:T(1,128)} %bitcast.48, ...), custom_call_target="tpu_custom_call" | custom-call | flops 64424509440 | bytes 25165824 | tf_op jit(solution)/shard_map/attention_backward/pallas_call | solution.py:811
  393.9 0.0 reduce-scatter.9.cloned.1.call-start
  394.0 0.5 reduce-scatter.9.cloned.1.call-update
  394.6 0.0 all-reduce.2.cloned.1.call-start
  394.7 0.5 all-reduce.2.cloned.1.call-update
  395.2 0.0 all-gather.10.cloned.1.call-start
  395.2 61.9 %reduce-scatter.5.cloned.1.call-done = bf16[96,1024]{1,0:T(8,128)(2,1)} async-done(((bf16[768,1024]{1,0:T(8,128)(2,1)}), bf16[96,1024]{1,0:T(8,128)(2,1)}) %reduce-scatter.5.cloned.1.call-update) | async-done | bytes 196624 | tf_op jit(solution)/shard_map/reduce_scatter | solution.py:916
  457.1 0.0 reduce-scatter.11.cloned.1.call-start
  457.2 121.0 %reduce-scatter.9.cloned.1.call-done = bf16[1,4,3,704,128]{4,3,2,1,0:T(8,128)(2,1)} async-done(((bf16[8,4,3,704,128]{4,3,2,1,0:T(8,128)(2,1)}), bf16[1,4,3,704,128]{4,3,2,1,0:T(8,128)(2,1)}) %reduce-scatter.9.cloned.1.call-update) | async-done | bytes 2162704 | tf_op jit(solution)/shard_map/reduce_scatter | solution.py:904
  578.2 9.5 %collective-permute-start.1 = (bf16[512,1024]{1,0:T(8,128)(2,1)}, bf16[512,1024]{1,0:T(8,128)(2,1)}, u32[]{:S(2)}, u32[]{:S(2)}) collective-permute-start(bf16[512,1024]{1,0:T(8,128)(2,1)} %get-tuple-element.35), channel_id=1, source_target_pairs={{0,0},{1,1},{2,4},{3,5},{4,2},{5,3},{6,6},{7,7},{8,8},{9,9},{10,12... | collective-permute-start | bytes 3145736 | tf_op jit(solution)/shard_map/ppermute | solution.py:902
  587.7 0.6 reduce_sum.39
  588.3 1.1 multiply_reduce_fusion
  589.5 1.6 convert_element_type.44
  591.1 0.2 convert_bitcast_fusion
  591.2 1.8 copy.29
  593.1 2.9 copy.30
  595.9 1.4 concatenate.11
  597.3 39.3 %psum.14 = f32[2050]{0:T(1024)S(1)} all-reduce(f32[2050]{0:T(1024)S(1)} %concatenate.11), channel_id=1, replica_groups=mesh['hi'=4,'core'=2,'zh'=2,'zq'=2] {'hi','core','zh','zq'}, use_global_device_ids=true, to_apply=%region_4.5 | all-reduce | flops 2050 | bytes 16400 | tf_op jit(solution)/shard_map/psum | solution.py:931
  636.6 0.5 fusion.8
  637.1 0.6 fusion.9
  637.7 2.1 convert_element_type.51
  639.9 46.0 %all-gather.10.cloned.1.call-done = bf16[1536,1024]{1,0:T(8,128)(2,1)} async-done(((bf16[96,1024]{1,0:T(8,128)(2,1)}), bf16[1536,1024]{1,0:T(8,128)(2,1)}) %all-gather.10.cloned.1.call-update) | async-done | bytes 3145744 | tf_op jit(solution)/shard_map/all_gather | solution.py:917
  685.9 1.5 constant_dynamic-slice_fusion
  687.4 2.1 convert.5
  689.5 42.4 %reduce-scatter.11.cloned.1.call-done = bf16[1,1,3,704,128]{4,3,2,1,0:T(8,128)(2,1)} async-done(((bf16[1,4,3,704,128]{4,3,2,1,0:T(8,128)(2,1)}), bf16[1,1,3,704,128]{4,3,2,1,0:T(8,128)(2,1)}) %reduce-scatter.11.cloned.1.call-update) | async-done | bytes 540688 | tf_op jit(solution)/shard_map/reduce_scatter | solution.py:905
  731.9 2.1 convert_bitcast_fusion.1
  734.0 2.3 copy.33
  (25 shorter events, 0.2 us)
Async XLA Ops:
  7.2 183.1 %all-gather.8.cloned.1.call-start = ((), (), s32[]{:S(2)}) async-start(), calls=%async_computation.10 | async-start | bytes 2621440 | tf_op jit(solution)/shard_map/all_gather | solution.py:865
  7.9 221.7 %all-gather.6.cloned.1.call-start = ((), (), s32[]{:S(2)}) async-start(), calls=%async_computation.4 | async-start | bytes 17842176 | tf_op jit(solution)/shard_map/all_gather | solution.py:864
  8.7 386.0 %reduce-scatter.7.cloned.1.call-start = ((), (), s32[]{:S(2)}) async-start(), calls=%async_computation.6 | async-start | bytes 2621440 | tf_op jit(solution)/shard_map/reduce_scatter | solution.py:907
  8.7 181.5 %collective-permute-start = (bf16[512,1024]{1,0:T(8,128)(2,1)}, bf16[512,1024]{1,0:T(8,128)(2,1)S(1)}, u32[]{:S(2)}, u32[]{:S(2)}) collective-permute-start(bf16[512,1024]{1,0:T(8,128)(2,1)} %param.17), channel_id=1, source_target_pairs={{0,0},{1,1},{2,4},{3,5},{4,2},{5,3},{6,6},{7,7},{8,8},{9,9},{10,12... | collective-permute-start | bytes 3145736 | tf_op jit(solution)/shard_map/ppermute | solution.py:879
  190.3 39.4 %copy-start.6 = (bf16[512,1024]{1,0:T(8,128)(2,1)}, bf16[512,1024]{1,0:T(8,128)(2,1)S(1)}, u32[]{:S(2)}) copy-start(bf16[512,1024]{1,0:T(8,128)(2,1)S(1)} %collective-permute-done.dy) | copy-start | bytes 3145732
  272.9 184.2 %reduce-scatter.5.cloned.1.call-start = ((), (), s32[]{:S(2)}) async-start(), calls=%async_computation.5 | async-start | bytes 1769472 | tf_op jit(solution)/shard_map/reduce_scatter | solution.py:916
  393.9 184.2 %reduce-scatter.9.cloned.1.call-start = ((), (), s32[]{:S(2)}) async-start(), calls=%async_computation.8 | async-start | bytes 19464192 | tf_op jit(solution)/shard_map/reduce_scatter | solution.py:904
  394.5 193.1 %copy-start.5 = (f32[8,256]{1,0:T(8,128)S(1)}, f32[8,256]{1,0:T(8,128)}, u32[]{:S(2)}) copy-start(f32[8,256]{1,0:T(8,128)} %get-tuple-element.47) | copy-start | bytes 24580
  394.5 193.7 %copy-start = (bf16[512,1024]{1,0:T(8,128)(2,1)S(1)}, bf16[512,1024]{1,0:T(8,128)(2,1)}, u32[]{:S(2)}) copy-start(bf16[512,1024]{1,0:T(8,128)(2,1)} %param.10) | copy-start | bytes 3145732
  394.6 194.9 %copy-start.4 = (f32[8,1024]{1,0:T(8,128)S(1)}, f32[8,1024]{1,0:T(8,128)}, u32[]{:S(2)}) copy-start(f32[8,1024]{1,0:T(8,128)} %get-tuple-element.45) | copy-start | bytes 98308
  394.6 194.9 %copy-start.3 = (f32[8,1024]{1,0:T(8,128)S(1)}, f32[8,1024]{1,0:T(8,128)}, u32[]{:S(2)}) copy-start(f32[8,1024]{1,0:T(8,128)} %get-tuple-element.46) | copy-start | bytes 98308
  394.6 194.9 %copy-start.2 = (bf16[512,1024]{1,0:T(8,128)(2,1)S(1)}, bf16[512,1024]{1,0:T(8,128)(2,1)}, u32[]{:S(2)}) copy-start(bf16[512,1024]{1,0:T(8,128)(2,1)} %get-tuple-element.43) | copy-start | bytes 3145732
  394.6 243.1 %all-reduce.2.cloned.1.call-start = ((), (), s32[]{:S(2)}) async-start(), calls=%async_computation.7 | async-start | bytes 1048576 | tf_op jit(solution)/shard_map/psum | solution.py:908
  395.2 290.7 %all-gather.10.cloned.1.call-start = ((), (), s32[]{:S(2)}) async-start(), calls=%async_computation.11 | async-start | bytes 3342336 | tf_op jit(solution)/shard_map/all_gather | solution.py:917
  457.1 274.7 %reduce-scatter.11.cloned.1.call-start = ((), (), s32[]{:S(2)}) async-start(), calls=%async_computation.9 | async-start | bytes 2703360 | tf_op jit(solution)/shard_map/reduce_scatter | solution.py:905
  578.2 59.5 %collective-permute-start.1 = (bf16[512,1024]{1,0:T(8,128)(2,1)}, bf16[512,1024]{1,0:T(8,128)(2,1)}, u32[]{:S(2)}, u32[]{:S(2)}) collective-permute-start(bf16[512,1024]{1,0:T(8,128)(2,1)} %get-tuple-element.35), channel_id=1, source_target_pairs={{0,0},{1,1},{2,4},{3,5},{4,2},{5,3},{6,6},{7,7},{8,8},{9,9},{10,12... | collective-permute-start | bytes 3145736 | tf_op jit(solution)/shard_map/ppermute | solution.py:902
  588.3 2.8 copy-start.1
Sparse Core Ops, SparseCore 0:
  9.6 77.8 all-gather.7
  90.2 139.3 all-gather.5
  273.1 54.9 reduce-scatter.6
  394.1 62.9 reduce-scatter.4
  460.6 117.5 reduce-scatter.8
  581.1 54.8 all-reduce.1
  638.3 47.5 all-gather.9
  688.2 43.6 reduce-scatter.10

commit v2 on v1

--- a/solution.py
+++ b/solution.py
@@ -427,17 +427,36 @@
 
 
 def mlp_kernel(
-    p_ref, x, ai, dy, g2, wo, wm, lo, gh, ga, dwm, dwo, gg2, hid, n2, acc_o, acc_g
+    xa, ai, dy, g2, wo, wm, lo, gh, ga, dsum, dosum, gg2,
+    x, hid, n2, acc_o, acc_g, buf, rcv, bo, rcvo, x_s, buf_s, buf_r, bo_s, bo_r,
 ):
     step = pl.program_id(0)
     n = ai.shape[0]
     wide = wm.shape[0]
-    width = x.shape[2]
+    width = x.shape[1]
     dw = width // wide
+    hi_n = wide // 2
+    rw = bo.shape[3]
+    h, c, r, q = coords()
+    own_x = pltpu.make_async_copy(xa.at[c * (n // 2) + q], x, x_s)
+    mate = (h, 1 - c, r, q)
+    slot = step % 2
+    last = n - 1
+
+    def to_mate(at):
+        return remote(buf.at[at, 1 - c], rcv.at[at], buf_s.at[at], buf_r.at[at], mate)
+
+    def out_to_mate():
+        return remote(bo.at[1 - c], rcvo, bo_s, bo_r, mate)
 
     @pl.when(step == 0)
     def _():
-        total = x[0].astype(F32)
+        own_x.start()
+        barrier = pltpu.get_barrier_semaphore()
+        pl.semaphore_signal(barrier, inc=1, device_id=mate, device_id_type=MESH)
+        pl.semaphore_wait(barrier, 1)
+        own_x.wait()
+        total = x[...].astype(F32)
         for s in range(n):
             total = total + nn(ai[s], wo[s])
         hid[...] = total
@@ -446,29 +465,35 @@
         acc_o[...] = jnp.zeros_like(acc_o)
         acc_g[...] = jnp.zeros_like(acc_g)
 
-    def weight(j):
-        return jnp.concatenate([wm[w, 0, j] for w in range(wide)], axis=1)
-
-    def put(j, grad):
-        low = grad.astype(BF)
-        for w in range(wide):
-            dwm[w, 0, j] = low[:, w * dw : (w + 1) * dw]
-
-    gate = nt(n2[...], weight(0))
-    up = nt(n2[...], weight(1))
-    sig = jax.nn.sigmoid(gate)
-    silu = gate * sig
-    inner = (silu * up).astype(BF)
-    grad_inner = nt(dy[...], weight(2))
-    grad_gate = (grad_inner * up * sig * (1.0 + gate * (1.0 - sig))).astype(BF)
-    grad_up = (grad_inner * silu).astype(BF)
-    acc_o[...] += nn(inner, weight(2))
-    acc_g[...] += nn(grad_gate, weight(0)) + nn(grad_up, weight(1))
-    put(0, tn(grad_gate, n2[...]))
-    put(1, tn(grad_up, n2[...]))
-    put(2, tn(inner, dy[...]))
-
-    @pl.when(step == pl.num_programs(0) - 1)
+    @pl.when(step < n)
+    def _():
+        @pl.when(step > 1)
+        def _():
+            to_mate(slot).wait_send()
+
+        def weight(j):
+            return jnp.concatenate([wm[w, 0, j] for w in range(wide)], axis=1)
+
+        def put(j, grad):
+            low = grad.astype(BF)
+            for w in range(wide):
+                buf[slot, w % 2, w // 2, j] = low[:, w * dw : (w + 1) * dw]
+
+        gate = nt(n2[...], weight(0))
+        up = nt(n2[...], weight(1))
+        sig = jax.nn.sigmoid(gate)
+        silu = gate * sig
+        inner = (silu * up).astype(BF)
+        grad_inner = nt(dy[...], weight(2))
+        grad_gate = (grad_inner * up * sig * (1.0 + gate * (1.0 - sig))).astype(BF)
+        grad_up = (grad_inner * silu).astype(BF)
+        acc_o[...] += nn(inner, weight(2))
+        acc_g[...] += nn(grad_gate, weight(0)) + nn(grad_up, weight(1))
+        put(0, tn(grad_gate, n2[...]))
+        put(1, tn(grad_up, n2[...]))
+        put(2, tn(inner, dy[...]))
+
+    @pl.when(step == last)
     def _():
         hidden = hid[...]
         lo[...] = (hidden + acc_o[...]).astype(BF)
@@ -482,71 +507,121 @@
         low = grad_h.astype(BF)
         for s in range(n):
             ga[s] = nt(low, wo[s]).astype(BF)
-            dwo[s] = tn(ai[s], low).astype(BF)
-
-
-def feed_forward(place, xa, ai, dy, g2, wo, wm):
+            grad_wo = tn(ai[s], low).astype(BF)
+            for w in range(wide):
+                bo[w % 2, w // 2, s] = grad_wo[w * rw : (w + 1) * rw]
+
+    @pl.when(step > 0)
+    def _():
+        before = (step + 1) % 2
+        to_mate(before).wait_recv()
+        for a in range(hi_n):
+            for j in range(3):
+                total = buf[before, c, a, j].astype(F32) + rcv[before, a, j].astype(F32)
+                dsum[a, 0, j] = total.astype(BF)
+
+    @pl.when(step < n)
+    def _():
+        to_mate(slot).start()
+
+    @pl.when(step == last)
+    def _():
+        out_to_mate().start()
+
+    @pl.when(step == n)
+    def _():
+        out_to_mate().wait_recv()
+        for a in range(hi_n):
+            for s in range(n):
+                total = bo[c, a, s].astype(F32) + rcvo[a, s].astype(F32)
+                dosum[a, s] = total.astype(BF)
+        out_to_mate().wait_send()
+        to_mate(0).wait_send()
+        if n > 1:
+            to_mate(1).wait_send()
+
+
+def feed_forward(xa, ai, dy, g2, wo, wm):
     n, tok, sw = ai.shape
     width = dy.shape[1]
     wide, _, _, ffs, dw = wm.shape
+    hi_n = wide // 2
+    rw = sw // wide
 
     def whole(*shape):
-        return pl.BlockSpec(shape, lambda i, p: (0,) * len(shape))
-
-    chunk = pl.BlockSpec((wide, 1, 3, ffs, dw), lambda i, p: (0, i, 0, 0, 0))
+        return pl.BlockSpec(shape, lambda i: (0,) * len(shape))
+
+    def fixed(*shape):
+        return pl.BlockSpec(
+            shape, lambda i: (0,) * len(shape), pipeline_mode=pl.Buffered(1)
+        )
+
     return pl.pallas_call(
         mlp_kernel,
         out_shape=(
             jax.ShapeDtypeStruct((tok, width), BF),
             jax.ShapeDtypeStruct((tok, width), F32),
             jax.ShapeDtypeStruct((n, tok, sw), BF),
-            jax.ShapeDtypeStruct(wm.shape, BF),
-            jax.ShapeDtypeStruct((n, sw, width), BF),
+            jax.ShapeDtypeStruct((hi_n, n, 3, ffs, dw), BF),
+            jax.ShapeDtypeStruct((hi_n, n, rw, width), BF),
             jax.ShapeDtypeStruct((8, width), F32),
         ),
-        grid_spec=pltpu.PrefetchScalarGridSpec(
-            num_scalar_prefetch=1,
-            grid=(n,),
+        grid_spec=pl.GridSpec(
+            grid=(n + 1,),
             in_specs=[
-                pl.BlockSpec((1, tok, width), lambda i, p: (p[0], 0, 0)),
-                whole(n, tok, sw),
-                whole(tok, width),
-                whole(1, width),
-                whole(n, sw, width),
-                chunk,
+                ANY,
+                fixed(n, tok, sw),
+                fixed(tok, width),
+                fixed(1, width),
+                fixed(n, sw, width),
+                pl.BlockSpec(
+                    (wide, 1, 3, ffs, dw), lambda i: (0, jnp.minimum(i, n - 1), 0, 0, 0)
+                ),
             ],
             out_specs=(
                 whole(tok, width),
                 whole(tok, width),
                 whole(n, tok, sw),
-                chunk,
-                whole(n, sw, width),
+                pl.BlockSpec(
+                    (hi_n, 1, 3, ffs, dw), lambda i: (0, jnp.maximum(i - 1, 0), 0, 0, 0)
+                ),
+                whole(hi_n, n, rw, width),
                 whole(8, width),
             ),
             scratch_shapes=[
+                pltpu.VMEM((tok, width), BF),
                 pltpu.VMEM((tok, width), F32),
                 pltpu.VMEM((tok, width), BF),
                 pltpu.VMEM((tok, width), F32),
                 pltpu.VMEM((tok, width), F32),
+                pltpu.VMEM((2, 2, hi_n, 3, ffs, dw), BF),
+                pltpu.VMEM((2, hi_n, 3, ffs, dw), BF),
+                pltpu.VMEM((2, hi_n, n, rw, width), BF),
+                pltpu.VMEM((hi_n, n, rw, width), BF),
+                DMA, DMA((2,)), DMA((2,)), DMA, DMA,
             ],
         ),
         name="feed_forward",
         compiler_params=pltpu.CompilerParams(
-            dimension_semantics=("arbitrary",), vmem_limit_bytes=VMEM_MAX
+            dimension_semantics=("arbitrary",),
+            collective_id=4,
+            has_side_effects=True,
+            vmem_limit_bytes=VMEM_MAX,
         ),
         cost_estimate=pl.CostEstimate(
             flops=18 * tok * width * ffs * n, bytes_accessed=40 << 20, transcendentals=tok * ffs * n
         ),
-    )(place, xa, ai, dy, g2, wo, wm)
+    )(xa, ai, dy, g2, wo, wm)
 
 
 def backward_kernel(
-    sizes, block, ga, xa, ws, g1, cos, sin, bias_ref, qi, ki, mi, ao, lse, gh,
-    gv, gi, dwq, gg1,
-    do, normed, dq, dk, dv, dcat, gow, gnp, rcv, rcv2, gis,
+    sizes, block, ga, ds, dos, lo, xa, ws, g1, cos, sin, bias_ref, qi, ki, mi, ao, lse, gh,
+    gv, gi, dwq, gg1, lo_in, rx, rxo, zr, zo,
+    do, normed, dq, dk, dv, dcat, gow, gnp, rcv, rcv2, gis, part, zs, zos, do_part,
     do_s, do_r, gv_s, gv_r, co_s, co_r, pe_s, pe_r, gi_s, gi_r, loc,
+    rx_s, rx_r, rxo_s, rxo_r, lo_s, lo_r, ld, z_s, z_r, zo_s, zo_r,
 ):
-    _, _, _, nh = sizes
+    hi_n, _, _, nh = sizes
     n = 2 * nh
     h, c, r, q = coords()
     p = c * nh + q
@@ -559,7 +634,88 @@
     halves = pw // HEAD_DIM
     same = c == r
     mate = (h, 1 - c, r, q)
-    greet_plane(sizes, False)
+    swap_to = (h, r, c, q)
+    zed = r * nh + q
+    greet_plane(sizes, True)
+
+    def over_hi(dh, i):
+        to = (h + dh) % hi_n
+        return remote(
+            ds.at[to, i], rx.at[dh - 1, i], rx_s.at[dh, i], rx_r.at[dh, i], (to, c, r, q)
+        )
+
+    def out_over_hi(dh):
+        to = (h + dh) % hi_n
+        return remote(dos.at[to], rxo.at[dh - 1], rxo_s.at[dh], rxo_r.at[dh], (to, c, r, q))
+
+    def send_lo():
+        return remote(lo, lo_in, lo_s, lo_r, swap_to)
+
+    def over_z(i):
+        return remote(zs.at[i], zr.at[zed], z_s.at[i], z_r.at[zed], (h, c, i // nh, i % nh))
+
+    def out_over_z(i):
+        return remote(zos.at[i], zo.at[zed], zo_s.at[i], zo_r.at[zed], (h, c, i // nh, i % nh))
+
+    def keep_z(i):
+        return pltpu.make_async_copy(zs.at[i], zr.at[i], z_s.at[i])
+
+    def keep_out_z(i):
+        return pltpu.make_async_copy(zos.at[i], zo.at[i], zo_s.at[i])
+
+    def load_chunk(i):
+        copies = [pltpu.make_async_copy(ds.at[h, i], part.at[0], ld.at[0])]
+        for dh in range(1, hi_n):
+            copies.append(pltpu.make_async_copy(rx.at[dh - 1, i], part.at[dh], ld.at[dh]))
+        return copies
+
+    def reduce_chunk(i):
+        for dh in range(1, hi_n):
+            over_hi(dh, i).wait_recv()
+        for copy in load_chunk(i):
+            copy.start()
+        for copy in load_chunk(i):
+            copy.wait()
+        for j in range(3):
+            total = part[0, j].astype(F32)
+            for dh in range(1, hi_n):
+                total = total + part[dh, j].astype(F32)
+            zs[i, j] = total.astype(BF)
+
+        @pl.when(zed != i)
+        def _():
+            over_z(i).start()
+
+        @pl.when(zed == i)
+        def _():
+            keep_z(i).start()
+
+    own_out = pltpu.make_async_copy(dos.at[h], zos, ld.at[0])
+
+    def reduce_out():
+        own_out.start()
+        own_out.wait()
+        for dh in range(1, hi_n):
+            out_over_hi(dh).wait_recv()
+            copy = pltpu.make_async_copy(rxo.at[dh - 1], do_part, ld.at[dh])
+            copy.start()
+            copy.wait()
+            zos[...] = (zos[...].astype(F32) + do_part[...].astype(F32)).astype(BF)
+        for i in range(n):
+            @pl.when(zed != i)
+            def _():
+                out_over_z(i).start()
+
+            @pl.when(zed == i)
+            def _():
+                keep_out_z(i).start()
+
+    @pl.when(c != r)
+    def _():
+        send_lo().start()
+
+    for dh in range(1, hi_n):
+        out_over_hi(dh).start()
 
     def send_do(s):
         to = (h, s // nh, r, s % nh)
@@ -572,6 +728,9 @@
             send_do(s).start()
 
     keep_do.start()
+    for i in range(n):
+        for dh in range(1, hi_n):
+            over_hi(dh, i).start()
     br = 256
 
     def norm(i, carry):
@@ -675,6 +834,9 @@
         return carry
 
     lax.fori_loop(0, pairs, pair_step, 0)
+    reduce_out()
+    for i in range(n - 1):
+        reduce_chunk(i)
 
     ck = min(256, tok)
     half_rows = row_len // 2
@@ -727,7 +889,8 @@
     for t in range(3):
         dwq[t * sw : (t + 1) * sw, :] = tn(dcat[t], normed[...]).astype(BF)
 
-    partner = (h, r, c, q)
+    reduce_chunk(n - 1)
+    partner = swap_to
     gg1[...] = jnp.zeros_like(gg1)
 
     def send_gi(k):
@@ -797,8 +960,30 @@
 
     lax.fori_loop(0, pairs, drain, 0)
 
-
-def attention_backward(sizes, ga, xa, ws, g1, cos, sin, bias, qi, ki, mi, ao, lse, gh):
+    @pl.when(c != r)
+    def _():
+        send_lo().wait_send()
+        send_lo().wait_recv()
+
+    for dh in range(1, hi_n):
+        out_over_hi(dh).wait_send()
+        for i in range(n):
+            over_hi(dh, i).wait_send()
+    for i in range(n):
+        @pl.when(zed != i)
+        def _():
+            over_z(i).wait_send()
+            out_over_z(i).wait_send()
+            remote(zs.at[i], zr.at[i], z_s.at[i], z_r.at[i], mate).wait_recv()
+            remote(zos.at[i], zo.at[i], zo_s.at[i], zo_r.at[i], mate).wait_recv()
+
+        @pl.when(zed == i)
+        def _():
+            keep_z(i).wait()
+            keep_out_z(i).wait()
+
+
+def attention_backward(sizes, ga, ds, dos, lo, xa, ws, g1, cos, sin, bias, qi, ki, mi, ao, lse, gh):
     _, _, _, nh = sizes
     n, tok, sw = ga.shape
     row_len, width = xa.shape
@@ -808,6 +993,10 @@
     ck = min(256, tok)
     n_half = row_len // 2 // ck
     n_blk = tok // ck
+    hi_n = sizes[0]
+    _, _, _, ffs, dw = ds.shape
+    rw = dos.shape[2]
+    others = max(hi_n - 1, 1)
     return pl.pallas_call(
         functools.partial(backward_kernel, sizes, block),
         out_shape=(
@@ -815,9 +1004,14 @@
             jax.ShapeDtypeStruct((tok, width), BF),
             jax.ShapeDtypeStruct((3 * sw, width), BF),
             jax.ShapeDtypeStruct((8, width), F32),
-        ),
-        in_specs=[ANY] + [VM] * 12,
-        out_specs=(ANY, ANY, VM, VM),
+            jax.ShapeDtypeStruct((tok, width), BF),
+            jax.ShapeDtypeStruct((others, n, 3, ffs, dw), BF),
+            jax.ShapeDtypeStruct((others, n, rw, width), BF),
+            jax.ShapeDtypeStruct((n, 3, ffs, dw), BF),
+            jax.ShapeDtypeStruct((n, rw, width), BF),
+        ),
+        in_specs=[ANY] * 4 + [VM] * 12,
+        out_specs=(ANY, ANY, VM, VM) + (ANY,) * 5,
         scratch_shapes=[
             pltpu.VMEM((n, tok, sw), BF),
             pltpu.VMEM((row_len, width), BF),
@@ -830,12 +1024,22 @@
             pltpu.VMEM((row_len // 2, width), BF),
             pltpu.VMEM((max(nh - 1, 1), tok, width), BF),
             pltpu.VMEM((tok, width), BF),
+            pltpu.VMEM((hi_n, 3, ffs, dw), BF),
+            pltpu.VMEM((n, 3, ffs, dw), BF),
+            pltpu.VMEM((n, rw, width), BF),
+            pltpu.VMEM((n, rw, width), BF),
             DMA((n,)), DMA((n,)),
             DMA((pairs, n)), DMA((pairs, n)),
             DMA((n_half,)), DMA((n_half,)),
             DMA((nh, n_blk)), DMA((nh, n_blk)),
             DMA((n_blk,)), DMA((n_blk,)),
             DMA((1 + pairs,)),
+            DMA((hi_n, n)), DMA((hi_n, n)),
+            DMA((hi_n,)), DMA((hi_n,)),
+            DMA, DMA,
+            DMA((hi_n,)),
+            DMA((n,)), DMA((n,)),
+            DMA((n,)), DMA((n,)),
         ],
         name="attention_backward",
         compiler_params=pltpu.CompilerParams(
@@ -844,7 +1048,187 @@
         cost_estimate=pl.CostEstimate(
             flops=60 << 30, bytes_accessed=24 << 20, transcendentals=row_len * row_len * sw // 128
         ),
-    )(ga, xa, ws, g1, cos, sin, bias, qi, ki, mi, ao, lse, gh)
+    )(ga, ds, dos, lo, xa, ws, g1, cos, sin, bias, qi, ki, mi, ao, lse, gh)
+
+
+def finish_kernel(
+    sizes, dwq, sm, zo, fin, og, total,
+    r1, s1, r2, s2, own, mine,
+    a_s, a_r, b_s, b_r, c_s, c_r, d_s, d_r, e_s, e_r, f_s, f_r, m_s, m_r,
+):
+    hi_n, _, _, nh = sizes
+    n = 2 * nh
+    h, c, r, q = coords()
+    wide = 2 * hi_n
+    w = 2 * h + c
+    mate = (h, 1 - c, r, q)
+    same = c == r
+    barrier = pltpu.get_barrier_semaphore()
+    count = 0
+    for dh in range(hi_n):
+        for dc in range(2):
+            if dh or dc:
+                to = ((h + dh) % hi_n, (c + dc) % 2, r, q)
+                pl.semaphore_signal(barrier, inc=1, device_id=to, device_id_type=MESH)
+                count += 1
+    for dc in range(2):
+        for dz in range(1, n):
+            to = (h, (c + dc) % 2, ((r * nh + q + dz) % n) // nh, ((r * nh + q + dz) % n) % nh)
+            pl.semaphore_signal(barrier, inc=1, device_id=to, device_id_type=MESH)
+            count += 1
+    pl.semaphore_wait(barrier, count)
+
+    def hi_part(dh):
+        to = (h + dh) % hi_n
+        return remote(dwq.at[to], r1.at[dh - 1], a_s.at[dh], a_r.at[dh], (to, c, r, q))
+
+    def hi_small(dh):
+        to = ((h + dh) % hi_n, c, r, q)
+        return remote(sm, s1.at[h], b_s.at[dh], b_r.at[dh], to)
+
+    for dh in range(1, hi_n):
+        hi_small(dh).start()
+    for dh in range(1, hi_n):
+        hi_part(dh).start()
+
+    out_rows = zo[0].astype(F32)
+    for i in range(1, n):
+        out_rows = out_rows + zo[i].astype(F32)
+    own[...] = out_rows.astype(BF)
+    og[w] = own[...]
+
+    def plane_out(dh, dc):
+        to = ((h + dh) % hi_n, (c + dc) % 2, r, q)
+        return remote(own, og.at[w], c_s.at[dh, dc], c_r.at[dh, dc], to)
+
+    for dh in range(hi_n):
+        for dc in range(2):
+            if dh or dc:
+                plane_out(dh, dc).start()
+
+    s1[h] = sm[...]
+    for dh in range(1, hi_n):
+        source = (h + hi_n - dh) % hi_n
+        remote(sm, s1.at[source], b_s.at[dh], b_r.at[dh], mate).wait_recv()
+    small = s1[0]
+    for i in range(1, hi_n):
+        small = small + s1[i]
+    spot = c * n + r * nh + q
+    s2[spot] = small
+
+    def plane_small(k):
+        dc, dz = k // n, k % n
+        z = (r * nh + q + dz) % n
+        to = (h, (c + dc) % 2, z // nh, z % nh)
+        return remote(s2.at[spot], s2.at[spot], d_s.at[k], d_r.at[k], to)
+
+    def small_arrives(k):
+        dc, dz = k // n, k % n
+        source = ((c + dc) % 2) * n + (r * nh + q + n - dz) % n
+        return remote(s2.at[source], s2.at[source], d_s.at[k], d_r.at[k], mate)
+
+    for k in range(1, 2 * n):
+        plane_small(k).start()
+
+    part = dwq[h].astype(F32)
+    for dh in range(1, hi_n):
+        hi_part(dh).wait_recv()
+        part = part + r1[dh - 1].astype(F32)
+    mine[...] = part.astype(BF)
+    across = remote(mine, r2, e_s, e_r, (h, c, 1 - r, q))
+
+    @pl.when(c != r)
+    def _():
+        across.start()
+
+    def spread(dh):
+        to = ((h + dh) % hi_n, c, r, q)
+        return remote(fin.at[h], fin.at[h], f_s.at[dh], f_r.at[dh], to)
+
+    def share(dh):
+        block = (h + hi_n - dh) % hi_n
+        return remote(fin.at[block], fin.at[block], m_s.at[dh], m_r.at[dh], mate)
+
+    @pl.when(same)
+    def _():
+        across.wait_recv()
+        fin[h] = (mine[...].astype(F32) + r2[...].astype(F32)).astype(BF)
+        for dh in range(1, hi_n):
+            spread(dh).start()
+        share(0).start()
+        for dh in range(1, hi_n):
+            block = (h + hi_n - dh) % hi_n
+            remote(fin.at[h], fin.at[block], f_s.at[dh], f_r.at[dh], mate).wait_recv()
+            share(dh).start()
+
+    for k in range(1, 2 * n):
+        small_arrives(k).wait_recv()
+    whole = s2[0]
+    for k in range(1, 2 * n):
+        whole = whole + s2[k]
+    total[...] = whole
+
+    @pl.when(c != r)
+    def _():
+        for dh in range(hi_n):
+            share(dh).wait_recv()
+        across.wait_send()
+
+    @pl.when(same)
+    def _():
+        for dh in range(1, hi_n):
+            spread(dh).wait_send()
+        for dh in range(hi_n):
+            share(dh).wait_send()
+
+    for dh in range(hi_n):
+        for dc in range(2):
+            if dh or dc:
+                theirs = 2 * ((h + hi_n - dh) % hi_n) + (c + dc) % 2
+                remote(own, og.at[theirs], c_s.at[dh, dc], c_r.at[dh, dc], mate).wait_recv()
+                plane_out(dh, dc).wait_send()
+    for dh in range(1, hi_n):
+        hi_small(dh).wait_send()
+        hi_part(dh).wait_send()
+    for k in range(1, 2 * n):
+        plane_small(k).wait_send()
+
+
+def finish(sizes, dwq, sm, zo):
+    hi_n, _, _, nh = sizes
+    n = 2 * nh
+    wide = 2 * hi_n
+    others = max(hi_n - 1, 1)
+    rw, width = zo.shape[1:]
+    return pl.pallas_call(
+        functools.partial(finish_kernel, sizes),
+        out_shape=(
+            jax.ShapeDtypeStruct(dwq.shape, BF),
+            jax.ShapeDtypeStruct((wide, rw, width), BF),
+            jax.ShapeDtypeStruct(sm.shape, F32),
+        ),
+        in_specs=[VM] * 3,
+        out_specs=(VM,) * 3,
+        scratch_shapes=[
+            pltpu.VMEM((others,) + dwq.shape[1:], BF),
+            pltpu.VMEM((hi_n,) + sm.shape, F32),
+            pltpu.VMEM(dwq.shape[1:], BF),
+            pltpu.VMEM((2 * n,) + sm.shape, F32),
+            pltpu.VMEM((rw, width), BF),
+            pltpu.VMEM(dwq.shape[1:], BF),
+            DMA((hi_n,)), DMA((hi_n,)),
+            DMA((hi_n,)), DMA((hi_n,)),
+            DMA((hi_n, 2)), DMA((hi_n, 2)),
+            DMA((2 * n,)), DMA((2 * n,)),
+            DMA, DMA,
+            DMA((hi_n,)), DMA((hi_n,)),
+            DMA((hi_n,)), DMA((hi_n,)),
+        ],
+        name="finish",
+        compiler_params=pltpu.CompilerParams(
+            collective_id=5, has_side_effects=True, vmem_limit_bytes=VMEM_MAX
+        ),
+    )(dwq, sm, zo)
 
 
 def per_device(sizes, layer_in, value_first, seg_start, gain_one, w_qkv, w_out, gain_two, w_mlp, grad_out):
@@ -858,7 +1242,6 @@
     row_len = n * tok
     short = row_len // seg_start.shape[0]
     h, c, r, q = coords()
-    place = (c * nh + q).astype(jnp.int32)
 
     w_mlp_t = jnp.transpose(w_mlp, (1, 2, 0)).reshape(3 * ffs, dw)
     wm = lax.all_gather(w_mlp_t, AXES, axis=0, tiled=False).reshape(wide, n, 3, ffs, dw)
@@ -898,47 +1281,34 @@
     ai, qo, ko, mo, ao, lse, own = attention_forward(
         sizes, xr, ws, va.reshape(row_len, sw), g1, cos, sin, bias
     )
-    lo, gh, ga, dwm, dwo, gg2 = feed_forward(place.reshape(1), xa, ai, dy, g2, wo, wm)
-    layer_out = lax.ppermute(lo, AXES, swap)
-
-    dwm = lax.psum_scatter(dwm, ("hi", "core"), scatter_dimension=0, tiled=True)
-    dwm = lax.psum_scatter(dwm, ("zh", "zq"), scatter_dimension=1, tiled=True)
-    grad_w_mlp = jnp.transpose(dwm.reshape(3, ffs, dw).astype(F32), (2, 0, 1))
-    dwo = lax.psum_scatter(dwo, ("zh", "zq"), scatter_dimension=0, tiled=True)
-    grad_w_out = lax.psum(dwo.reshape(sw, width), ("hi", "core")).astype(F32)
-
-    gv, gi, dwq, gg1 = attention_backward(
-        sizes, ga, xr, ws, g1, cos, sin, bias, qo, ko, mo, ao, lse, gh
+    lo, gh, ga, ds, dos, gg2 = feed_forward(xa, ai, dy, g2, wo, wm)
+    gv, gi, dwq, gg1, lo_in, _, _, zr, zo = attention_backward(
+        sizes, ga, ds, dos, lo, xr, ws, g1, cos, sin, bias, qo, ko, mo, ao, lse, gh
     )
+    first_f = value_first.astype(F32)
+    lane = jnp.arange(width)
+    third = jnp.where(
+        lane == 0, jnp.sum(first_f * first_f), jnp.where(lane == 1, jnp.sum(own), 0.0)
+    )
+    small = jnp.stack([jnp.sum(gg1, axis=0), jnp.sum(gg2, axis=0), third] + [jnp.zeros_like(third)] * 5)
+    fin, og, sums = finish(sizes, dwq.reshape(hi_n, 3 * sw // hi_n, width), small, zo)
+
+    layer_out = jnp.where(c == r, lo, lo_in)
     grad_value_first = gv.transpose(1, 0, 2).reshape(tok, width).astype(F32)
     grad_in = gi.astype(F32)
-
-    dwq = lax.psum_scatter(dwq, ("hi", "zh"), scatter_dimension=0, tiled=True)
-    dwq = lax.all_gather(dwq, ("core", "hi", "zh"), axis=0, tiled=False)
-    dwq = dwq.reshape(2, 3 * sw, width)
-    grad_w_qkv = lax.dynamic_index_in_dim(dwq, r, 0, keepdims=False)
-    grad_w_qkv = grad_w_qkv.reshape(3, sw, width).astype(F32)
-
-    first_f = value_first.astype(F32)
-    sums = jnp.concatenate(
-        [
-            jnp.sum(gg1, axis=0),
-            jnp.sum(gg2, axis=0),
-            jnp.sum(first_f * first_f).reshape(1),
-            jnp.sum(own).reshape(1),
-        ]
-    )
-    sums = lax.psum(sums, AXES)
+    grad_w_mlp = jnp.transpose(jnp.sum(zr.astype(F32), axis=0), (2, 0, 1))
+    grad_w_out = og.reshape(sw, width).astype(F32)
+    grad_w_qkv = fin.reshape(3, sw, width).astype(F32)
     entries = tok * width * wide * n
-    value_norms = jnp.sqrt(sums[2 * width :] / entries)
+    value_norms = jnp.sqrt(sums[2, :2] / entries)
     return (
         layer_out,
         grad_in,
         grad_value_first,
-        sums[:width],
+        sums[0],
         grad_w_qkv,
         grad_w_out,
-        sums[width : 2 * width],
+        sums[1],
         grad_w_mlp,
         value_norms,
     )

time: 750 us -> 537 us (0.72)
  waiting for transfers between devices: 313 us -> 5.95 us
  Pallas kernels: 329 us -> 464 us
  blocking collectives: 39.3 us -> 0 us
    reduce_scatter x4 -> x0, waiting for transfers between devices: 225 us -> none  [the longest x1 121 us: per_device(): dwm = lax.psum_scatter(dwm, ('hi', 'core'), scatter_dimension=0, tiled=True)]
    pallas_call x0 -> x1, Pallas kernels: none -> 75 us  [finish(): pl.pallas_call(functools.partial(finish_kernel, sizes), out_shape=(jax.Sh...]
    all_gather x1 -> x0, waiting for transfers between devices: 46 us -> none  [per_device(): dwq = lax.all_gather(dwq, ('core', 'hi', 'zh'), axis=0, tiled=False)]
    psum x1 -> x0, blocking collectives: 39.3 us -> none  [per_device(): sums = lax.psum(sums, AXES)]
    all_gather x1, waiting for transfers between devices: 39.4 us -> 4.55 us  [per_device(): lax.all_gather(w_mlp_t, AXES, axis=0, tiled=False)]
    pallas_call x1, Pallas kernels: 46.6 us -> 78 us  [attention_forward(): pl.pallas_call(functools.partial(forward_kernel, sizes, block), out_shape...]
    pallas_call x1, Pallas kernels: 121 us -> 147 us  [attention_backward(): pl.pallas_call(functools.partial(backward_kernel, sizes, block), out_shap...]
    ppermute x1 -> x0, starting transfers between devices: 9.49 us -> none  [per_device(): layer_out = lax.ppermute(lo, AXES, swap)]
  transfers between devices with their start and end apart: 10 -> 3, of which waited for: 5 -> 1; matrix products, arithmetic and copies ran while one was open for 4% -> 3% of each run, Pallas kernels for 38% -> 36%
where the time goes in v2:
time: 537 us; the launch traced here: 530 us
  Pallas kernels  464 us (86%)
  other arithmetic  21.3 us (4%)
  between operations  15.9 us (3%)
  local copies, waits for them, and re-layouts  13.5 us (3%)
  starting transfers between devices  9.52 us (2%)
  waiting for transfers between devices  5.95 us (1%)
    pallas_call x1, Pallas kernels, attention_backward(): pl.pallas_call(functools.partial(backward_kernel, sizes, block), out_shap...  147 us
    pallas_call x1, Pallas kernels, exchange_inputs(): pl.pallas_call(functools.partial(exchange_kernel, sizes, chunks), out_sha...  112 us
    pallas_call x1, Pallas kernels, attention_forward(): pl.pallas_call(functools.partial(forward_kernel, sizes, block), out_shape...  78 us
    pallas_call x1, Pallas kernels, finish(): pl.pallas_call(functools.partial(finish_kernel, sizes), out_shape=(jax.Sh...  75 us
    pallas_call x1, Pallas kernels, feed_forward(): pl.pallas_call(mlp_kernel, out_shape=(jax.ShapeDtypeStruct((tok, width),...  52.2 us
  transfers between devices with their start and end apart: 3, of which 1 were waited for; matrix products, arithmetic and copies ran while one was open for 3% of the time, Pallas kernels for 36%

profile of v2, /device:TPU:0, one launch (start us, length us, event | category | flops | bytes accessed | tf_op | source)
XLA Modules:
  0.0 530.2 jit_solution(16822636838129909023)
XLA Ops:
  7.2 0.0 all-gather.6.cloned.1.call-start
  7.2 0.7 all-gather.6.cloned.1.call-update
  7.9 0.0 all-gather.4.cloned.1.call-start
  8.0 0.7 all-gather.4.cloned.1.call-update
  8.7 0.0 copy-start.8
  8.7 9.4 %collective-permute-start = (bf16[512,1024]{1,0:T(8,128)(2,1)}, bf16[512,1024]{1,0:T(8,128)(2,1)}, u32[]{:S(2)}, u32[]{:S(2)}) collective-permute-start(bf16[512,1024]{1,0:T(8,128)(2,1)} %param.17), channel_id=1, source_target_pairs={{0,0},{1,1},{2,4},{3,5},{4,2},{5,3},{6,6},{7,7},{8,8},{9,9},{10,12... | collective-permute-start | bytes 3145736 | tf_op jit(solution)/shard_map/ppermute | solution.py:1262
  18.1 1.5 copy.26
  19.6 1.3 copy.27
  21.0 0.0 copy-done.8
  21.0 0.6 slice.15
  22.2 0.6 broadcast_in_dim.26.sg
  22.8 111.7 %exchange_inputs.1 = (bf16[4,512,1024]{2,1,0:T(8,128)(2,1)}, bf16[4,512,256]{2,1,0:T(8,128)(2,1)}, bf16[4,192,1024]{2,1,0:T(8,128)(2,1)}, f32[8,128]{1,0:T(8,128)}) custom-call(bf16[512,1024]{1,0:T(8,128)(2,1)} %x.1, bf16[4,512,256]{2,1,0:T(8,128)(2,1)} %bitcast.34, bf16[4,192,1024]{2,1,0:T(8,128)(2,1)} %bitcast.35, f32[8,128]{1,0:T(8,128)} %broadcast_in_dim.26.sg), custom_call_target="tpu_custom_call" | custom-call | bytes 167772160 | tf_op jit(solution)/shard_map/exchange_inputs/pallas_call | solution.py:246
  134.5 1.2 slice.16
  136.4 3.7 fusion
  140.1 3.0 pad_maximum_fusion
  143.1 0.6 mul.49.bias_ref
  143.7 0.0 copy-start
  143.7 78.0 %attention_forward.1 = (bf16[4,512,256]{2,1,0:T(8,128)(2,1)}, bf16[2048,256]{1,0:T(8,128)(2,1)}, bf16[2048,256]{1,0:T(8,128)(2,1)}, bf16[2048,256]{1,0:T(8,128)(...) custom-call(bf16[2048,1024]{1,0:T(8,128)(2,1)} %bitcast.45, ...), custom_call_target="tpu_custom_call" | custom-call | flops 21474836480 | bytes 16777216 | tf_op jit(solution)/shard_map/attention_forward/pallas_call | solution.py:405
  221.7 1.3 reduce_sum.48
  223.0 0.0 copy-done
  223.0 1.1 multiply_reduce_fusion
  224.1 1.3 compare_select_fusion.1
  225.4 0.0 collective-permute-done.dy
  225.4 0.0 all-gather.6.cloned.1.call-done
  225.5 4.6 all-gather.4.cloned.1.call-done
  230.0 52.2 %feed_forward.1 = (bf16[512,1024]{1,0:T(8,128)(2,1)}, f32[512,1024]{1,0:T(8,128)}, bf16[4,512,256]{2,1,0:T(8,128)(2,1)}, bf16[4,4,3,704,128]{4,3,2,1,0:T(8,128)(...) custom-call(bf16[4,512,1024]{2,1,0:T(8,128)(2,1)} %get-tuple-element.36.xa, ...), custom_call_target="tpu_custom_call" | custom-call | flops 26575110144 | bytes 41943040 | tf_op jit(solution)/shard_map/feed_forward/pallas_call | solution.py:559
  282.3 0.0 copy-start.7
  282.3 147.2 %attention_backward.1 = (bf16[4,512,256]{2,1,0:T(8,128)(2,1)}, bf16[512,1024]{1,0:T(8,128)(2,1)}, bf16[768,1024]{1,0:T(8,128)(2,1)}, f32[8,1024]{1,0:T(8,128)}, ...) custom-call(bf16[4,512,256]{2,1,0:T(8,128)(2,1)} %get-tuple-element., ...), custom_call_target="tpu_custom_call" | custom-call | flops 64424509440 | bytes 25165824 | tf_op jit(solution)/shard_map/attention_backward/pallas_call | solution.py:1000
  429.5 0.8 reduce_sum.45
  430.3 0.0 copy-done.7
  430.3 0.7 stack.16.sm
  431.0 75.0 %finish.1 = (bf16[4,192,1024]{2,1,0:T(8,128)(2,1)}, bf16[8,32,1024]{2,1,0:T(8,128)(2,1)}, f32[8,1024]{1,0:T(8,128)}) custom-call(bf16[4,192,1024]{2,1,0:T(8,128)(2,1)} %bitcast.36, f32[8,1024]{1,0:T(8,128)} %stack.16.sm, bf16[4,32,1024]{2,1,0:T(8,128)(2,1)} %get-tuple-element.58.zo), custom_call_target="tpu_custom_call" | custom-call | tf_op jit(solution)/shard_map/finish/pallas_call | solution.py:1203
  505.9 1.4 fusion.8
  507.4 1.2 sqrt_bitcast_fusion
  508.6 3.6 convert.4
  512.2 0.0 copy-done.6
  512.2 1.1 bitcast_convert_fusion
  513.3 0.0 copy-done.3
  513.3 0.2 convert_bitcast_fusion
  513.5 1.8 copy.29
  515.3 3.0 copy.30
  518.3 0.0 copy-done.2
  518.3 1.6 convert_element_type.46
  519.8 0.8 copy-done.1
  520.6 1.3 convert_reduce_fusion
  521.9 0.0 copy-done.4
  521.9 0.0 copy-done.5
  521.9 1.1 broadcast_select_fusion
  (11 shorter events, 0.1 us)
Async XLA Ops:
  7.2 218.3 %all-gather.6.cloned.1.call-start = ((), (), s32[]{:S(2)}) async-start(), calls=%async_computation.1 | async-start | bytes 2621440 | tf_op jit(solution)/shard_map/all_gather | solution.py:1248
  7.9 222.1 %all-gather.4.cloned.1.call-start = ((), (), s32[]{:S(2)}) async-start(), calls=%async_computation | async-start | bytes 17842176 | tf_op jit(solution)/shard_map/all_gather | solution.py:1247
  8.7 12.3 %copy-start.8 = (s32[2]{0:T(128)S(1)}, s32[2]{0:T(128)}, u32[]{:S(2)}) copy-start(s32[2]{0:T(128)} %param.11) | copy-start | bytes 28
  8.7 216.8 %collective-permute-start = (bf16[512,1024]{1,0:T(8,128)(2,1)}, bf16[512,1024]{1,0:T(8,128)(2,1)}, u32[]{:S(2)}, u32[]{:S(2)}) collective-permute-start(bf16[512,1024]{1,0:T(8,128)(2,1)} %param.17), channel_id=1, source_target_pairs={{0,0},{1,1},{2,4},{3,5},{4,2},{5,3},{6,6},{7,7},{8,8},{9,9},{10,12... | collective-permute-start | bytes 3145736 | tf_op jit(solution)/shard_map/ppermute | solution.py:1262
  143.7 79.3 %copy-start = (bf16[512,1024]{1,0:T(8,128)(2,1)S(1)}, bf16[512,1024]{1,0:T(8,128)(2,1)}, u32[]{:S(2)}) copy-start(bf16[512,1024]{1,0:T(8,128)(2,1)} %param.10) | copy-start | bytes 3145732
  282.3 148.0 %copy-start.7 = (f32[8,1024]{1,0:T(8,128)S(1)}, f32[8,1024]{1,0:T(8,128)}, u32[]{:S(2)}) copy-start(f32[8,1024]{1,0:T(8,128)} %get-tuple-element.56) | copy-start | bytes 98308
  508.6 3.6 copy-start.6
  508.6 4.7 copy-start.3
  515.3 3.0 copy-start.2
  518.3 2.4 copy-start.1
  519.8 2.1 copy-start.4
  519.8 2.1 copy-start.5
Sparse Core Ops, SparseCore 0:
  9.6 75.8 all-gather.5
  88.2 141.7 all-gather.3

commit v3 on v2

--- a/solution.py
+++ b/solution.py
@@ -2,6 +2,7 @@
 
 import jax
 import jax.numpy as jnp
+import numpy as np
 from jax import lax
 from jax.experimental import pallas as pl
 from jax.experimental.pallas import tpu as pltpu
@@ -79,19 +80,54 @@
     return slice(0, sw) if pw == sw else pl.ds(pl.multiple_of(pair * pw, pw), pw)
 
 
+def rope_rows(lo_c, lo_s, hi_c, hi_s, flag, i, rows):
+    step = lo_c.shape[0]
+    half = hi_c.shape[0] // 2
+    cos, sin = [], []
+    for u in range(rows // step):
+        k = i * (rows // step) + u
+        far, near = pl.ds(k, 1), pl.ds(k % half, 1)
+        ch = hi_c[near, :] * flag + hi_c[far, :] * (1.0 - flag)
+        sh = hi_s[near, :] * flag + hi_s[far, :] * (1.0 - flag)
+        cos.append(lo_c[...] * ch - lo_s[...] * sh)
+        sin.append(lo_s[...] * ch + lo_c[...] * sh)
+    cos = jnp.concatenate(cos, axis=0)
+    sin = jnp.concatenate(sin, axis=0)
+    return cos, jnp.where(first_lanes(rows, cos.shape[1]), -sin, sin)
+
+
+def rope_parts(row_len, pw):
+    half = HEAD_DIM // 2
+    frequency = 10000.0 ** (-2.0 * np.arange(half) / HEAD_DIM)
+    frequency = np.tile(frequency, pw // half)[None, :]
+    lo = np.arange(64)[:, None] * frequency
+    hi = 64.0 * np.arange(row_len // 64)[:, None] * frequency
+    return tuple(jnp.asarray(t, F32) for t in (np.cos(lo), np.sin(lo), np.cos(hi), np.sin(hi)))
+
+
+def columns_of(ref, s, sw):
+    if len(ref.shape) == 3:
+        return ref.at[s]
+    start = s * sw if isinstance(s, int) else pl.multiple_of(s * sw, sw)
+    return ref.at[:, pl.ds(start, sw)]
+
+
 def tiled(table, width):
     times = width // table.shape[1]
     return table if times == 1 else jnp.concatenate([table] * times, axis=1)
 
 
 def exchange_kernel(
-    sizes, chunks, x, v, w, sg, xa, va, ws, so, xs, wb, sb, vb,
-    swap_s, swap_r, peer_s, peer_r, core_s, core_r, w_s, w_r, wh_s, wh_r, sg_s, sg_r, v_s, v_r, loc,
+    sizes, chunks, x, w, sg, wt, wo, xa, ws, so, g1, cross, oz,
+    xs, wb, sb, tb, ob,
+    swap_s, swap_r, peer_s, peer_r, core_s, core_r, w_s, w_r, wh_s, wh_r, sg_s, sg_r, loc,
+    oz_s, oz_r, gp_s, gp_r, gh_s, gh_r, cr_s, cr_r,
 ):
     hi_n, _, _, nh = sizes
     n = 2 * nh
     h, c, r, q = coords()
     p = c * nh + q
+    zed = r * nh + q
     partner_p = r * nh + q
     rows = x.shape[0] // chunks
     same = c == r
@@ -127,14 +163,38 @@
     def send_sg():
         return remote(sg, so, sg_s, sg_r, partner)
 
-    local_x_in = pltpu.make_async_copy(x, xs, loc.at[0])
-    local_w_in = pltpu.make_async_copy(w, wb, loc.at[1])
-    local_s_in = pltpu.make_async_copy(sg, sb, loc.at[2])
-    local_v_in = pltpu.make_async_copy(v.at[p], vb, loc.at[3])
-    local_x_out = pltpu.make_async_copy(xs, xa.at[p], loc.at[4])
-    local_w_out = pltpu.make_async_copy(wb, ws, loc.at[5])
-    local_s_out = pltpu.make_async_copy(sb, so, loc.at[6])
-    local_v_out = pltpu.make_async_copy(vb, va.at[p], loc.at[7])
+    def shard_peer(dq):
+        to = (h, c, r, (q + dq) % nh)
+        return remote(wt, g1.at[h, (nh - dq) % nh], gp_s.at[dq], gp_r.at[dq], to)
+
+    def shard_hi(src, dh, t):
+        to = ((h + dh) % hi_n, c, r, q)
+        return remote(src, g1.at[h, t], gh_s.at[dh, t], gh_r.at[dh, t], to)
+
+    def shard_cross():
+        return remote(wt, cross, cr_s, cr_r, (h, c, 1 - r, q))
+
+    def rows_z(dz):
+        z = (zed + dz) % n
+        return remote(
+            wo.at[2 * h + c], oz.at[zed], oz_s.at[dz], oz_r.at[dz], (h, c, z // nh, z % nh)
+        )
+
+    def from_hi(dh):
+        return (h + hi_n - dh) % hi_n
+
+    local = [
+        (pltpu.make_async_copy(wt, tb, loc.at[0]), pltpu.make_async_copy(tb, g1.at[h, 0], loc.at[5])),
+        (
+            pltpu.make_async_copy(wo.at[2 * h + c], ob, loc.at[1]),
+            pltpu.make_async_copy(ob, oz.at[zed], loc.at[6]),
+        ),
+    ]
+    local_same = [
+        (pltpu.make_async_copy(x, xs, loc.at[2]), pltpu.make_async_copy(xs, xa.at[p], loc.at[7])),
+        (pltpu.make_async_copy(w, wb, loc.at[3]), pltpu.make_async_copy(wb, ws, loc.at[8])),
+        (pltpu.make_async_copy(sg, sb, loc.at[4]), pltpu.make_async_copy(sb, so, loc.at[9])),
+    ]
 
     @pl.when(other)
     def _():
@@ -149,10 +209,30 @@
             for dq in range(1, nh):
                 push_peer(x.at[part(k)], k, dq).start()
             push_mate(x.at[part(k)], k, 0).start()
-        local_x_in.start()
-        local_w_in.start()
-        local_s_in.start()
-        local_v_in.start()
+        for get, _ in local_same:
+            get.start()
+
+    for dq in range(1, nh):
+        shard_peer(dq).start()
+    for dh in range(1, hi_n):
+        shard_hi(wt, dh, 0).start()
+    for dz in range(1, n):
+        rows_z(dz).start()
+    shard_cross().start()
+    for get, _ in local:
+        get.start()
+
+    @pl.when(other)
+    def _():
+        send_w().wait_recv()
+        for dh in range(1, hi_n):
+            spread_w(dh).start()
+
+    for dq in range(1, nh):
+        remote(wt, g1.at[h, (nh - dq) % nh], gp_s.at[dq], gp_r.at[dq], mate).wait_recv()
+        t = (nh - dq) % nh
+        for dh in range(1, hi_n):
+            shard_hi(g1.at[h, t], dh, t).start()
 
     @pl.when(other)
     def _():
@@ -161,29 +241,16 @@
             for dq in range(1, nh):
                 push_peer(xa.at[p, part(k)], k, dq).start()
             push_mate(xa.at[p, part(k)], k, 0).start()
-        send_w().wait_recv()
-        for dh in range(1, hi_n):
-            spread_w(dh).start()
+
+    for get, put in local:
+        get.wait()
+        put.start()
 
     @pl.when(same)
     def _():
-        local_x_in.wait()
-        local_x_out.start()
-        local_w_in.wait()
-        local_w_out.start()
-        local_s_in.wait()
-        local_s_out.start()
-        local_v_in.wait()
-        local_v_out.start()
-
-    def send_v(s):
-        to = (h, s // nh, c, s % nh)
-        return remote(v.at[s], va.at[r * nh + q], v_s.at[s], v_r.at[r * nh + q], to)
-
-    for s in range(n):
-        @pl.when(jnp.logical_or(other, p != s))
-        def _():
-            send_v(s).start()
+        for get, put in local_same:
+            get.wait()
+            put.start()
 
     for k in range(chunks):
         for dq in range(1, nh):
@@ -204,7 +271,7 @@
     def _():
         send_sg().wait_recv()
         for dh in range(1, hi_n):
-            source = (h + hi_n - dh) % hi_n
+            source = from_hi(dh)
             remote(ws.at[source], ws.at[source], wh_s.at[dh], wh_r.at[dh], mate).wait_recv()
         send_sg().wait_send()
         send_w().wait_send()
@@ -213,16 +280,6 @@
         for k in range(chunks):
             swap_x(k).wait_send()
 
-    for b in range(n):
-        @pl.when(jnp.logical_or(other, p != b))
-        def _():
-            remote(v.at[0], va.at[b], v_s.at[b], v_r.at[b], mate).wait_recv()
-
-    for s in range(n):
-        @pl.when(jnp.logical_or(other, p != s))
-        def _():
-            send_v(s).wait_send()
-
     for k in range(chunks):
         for dq in range(1, nh):
             push_peer(x.at[part(k)], k, dq).wait_send()
@@ -231,46 +288,64 @@
 
     @pl.when(same)
     def _():
-        local_x_out.wait()
-        local_w_out.wait()
-        local_s_out.wait()
-        local_v_out.wait()
-
-
-def exchange_inputs(sizes, x, v, w, sg):
+        for _, put in local_same:
+            put.wait()
+
+    for dq in range(1, nh):
+        shard_peer(dq).wait_send()
+    for dz in range(1, n):
+        z = (zed + n - dz) % n
+        remote(wo.at[0], oz.at[z], oz_s.at[dz], oz_r.at[dz], mate).wait_recv()
+        rows_z(dz).wait_send()
+    for t in range(nh):
+        for dh in range(1, hi_n):
+            shard_hi(wt, dh, t).wait_send()
+            remote(wt, g1.at[from_hi(dh), t], gh_s.at[dh, t], gh_r.at[dh, t], mate).wait_recv()
+    shard_cross().wait_recv()
+    shard_cross().wait_send()
+    for _, put in local:
+        put.wait()
+
+
+def exchange_inputs(sizes, x, w, sg, wt, wo):
     hi_n, _, _, nh = sizes
     n = 2 * nh
     tok, width = x.shape
-    sw = v.shape[2]
     chunks = 4 if tok % 64 == 0 else 1
     return pl.pallas_call(
         functools.partial(exchange_kernel, sizes, chunks),
         out_shape=(
             jax.ShapeDtypeStruct((n, tok, width), BF),
-            jax.ShapeDtypeStruct((n, tok, sw), BF),
             jax.ShapeDtypeStruct(w.shape, BF),
             jax.ShapeDtypeStruct(sg.shape, F32),
+            jax.ShapeDtypeStruct((hi_n, nh) + wt.shape, BF),
+            jax.ShapeDtypeStruct(wt.shape, BF),
+            jax.ShapeDtypeStruct((n,) + wo.shape[1:], BF),
         ),
-        in_specs=[ANY] * 4,
-        out_specs=(ANY,) * 4,
+        in_specs=[ANY] * 5,
+        out_specs=(ANY,) * 6,
         scratch_shapes=[
             pltpu.VMEM((tok, width), BF),
             pltpu.VMEM(w.shape, BF),
             pltpu.VMEM(sg.shape, F32),
-            pltpu.VMEM((tok, sw), BF),
+            pltpu.VMEM(wt.shape, BF),
+            pltpu.VMEM(wo.shape[1:], BF),
             DMA((chunks,)), DMA((chunks,)),
             DMA((nh, chunks)), DMA((nh, chunks)),
             DMA((nh, chunks)), DMA((nh, chunks)),
             DMA, DMA,
             DMA((hi_n,)), DMA((hi_n,)),
             DMA, DMA,
+            DMA((10,)),
             DMA((n,)), DMA((n,)),
-            DMA((8,)),
+            DMA((nh,)), DMA((nh,)),
+            DMA((hi_n, nh)), DMA((hi_n, nh)),
+            DMA, DMA,
         ],
         name="exchange_inputs",
         compiler_params=pltpu.CompilerParams(collective_id=1, has_side_effects=True),
         cost_estimate=pl.CostEstimate(flops=0, bytes_accessed=160 << 20, transcendentals=0),
-    )(x, v, w, sg)
+    )(x, w, sg, wt, wo)
 
 
 def masked(scores, diagonal, crossing, causal, bias):
@@ -282,22 +357,78 @@
 
 
 def forward_kernel(
-    sizes, block, xa, ws, va, g1, cos, sin, bias_ref,
-    ai, qo, ko, mo, ao, lse, own, att_s, att_r, loc,
+    sizes, block, v, gout, cross, oz, xa, ws, g1, lo_c, lo_s, hi_c, hi_s, seg,
+    ai, dy_in, g2, oh, qo, ko, mo, ao, lse, own,
+    va, own_rows, tb, ob,
+    att_s, att_r, loc, v_s, v_r, dy_s, dy_r, gp_s, gp_r, gh_s, gh_r, oh_s, oh_r, lc,
 ):
-    _, _, _, nh = sizes
+    hi_n, _, _, nh = sizes
     n = 2 * nh
     h, c, r, q = coords()
     p = c * nh + q
-    row_len, sw = va.shape
+    row_len, sw = qo.shape
     tok = row_len // n
     short = row_len // 2
-    pw = cos.shape[1]
+    pw = lo_c.shape[1]
     pairs = sw // pw
     halves = pw // HEAD_DIM
-    greet_plane(sizes, False)
+    mate = (h, 1 - c, r, q)
+    other = c != r
+    greet_plane(sizes, True)
+
+    def send_v(s):
+        to = (h, s // nh, c, s % nh)
+        spot = r * nh + q
+        return remote(columns_of(v, s, sw), va.at[spot], v_s.at[s], v_r.at[spot], to)
+
+    def send_dy():
+        return remote(gout, dy_in, dy_s, dy_r, (h, r, c, q))
+
+    def shard_peer(dq):
+        to = (h, c, r, (q + dq) % nh)
+        return remote(cross, g2.at[h, (nh - dq) % nh], gp_s.at[dq], gp_r.at[dq], to)
+
+    def shard_hi(src, dh, t):
+        to = ((h + dh) % hi_n, c, r, q)
+        return remote(src, g2.at[h, t], gh_s.at[dh, t], gh_r.at[dh, t], to)
+
+    def rows_hi(dh):
+        to = ((h + dh) % hi_n, c, r, q)
+        return remote(oz, oh.at[h], oh_s.at[dh], oh_r.at[dh], to)
+
+    def from_hi(dh):
+        return (h + hi_n - dh) % hi_n
+
+    keep_v = pltpu.make_async_copy(columns_of(v, p, sw), va.at[p], lc.at[0])
+    local = [
+        (pltpu.make_async_copy(cross, tb, lc.at[1]), pltpu.make_async_copy(tb, g2.at[h, 0], lc.at[3])),
+        (pltpu.make_async_copy(oz, ob, lc.at[2]), pltpu.make_async_copy(ob, oh.at[h], lc.at[4])),
+    ]
+    for s in range(n):
+        @pl.when(jnp.logical_or(other, p != s))
+        def _():
+            send_v(s).start()
+
+    @pl.when(c == r)
+    def _():
+        keep_v.start()
+
+    for dq in range(1, nh):
+        shard_peer(dq).start()
+    for dh in range(1, hi_n):
+        rows_hi(dh).start()
+        shard_hi(cross, dh, 0).start()
+
+    @pl.when(other)
+    def _():
+        send_dy().start()
+
+    for get, _ in local:
+        get.start()
+
     br = 256
     own[...] = jnp.zeros_like(own)
+    flag = seg[0:1, 0:1]
 
     def project(i, carry):
         rows = pl.ds(pl.multiple_of(i * br, br), br)
@@ -306,21 +437,43 @@
         normed = (xf * inv * g1[...]).astype(BF)
         raw = nt(normed, ws[...])
         first = first_lanes(br, sw)
-        ct = tiled(cos[rows, :], sw)
-        st = tiled(sin[rows, :], sw)
+        ct, st = rope_rows(lo_c, lo_s, hi_c, hi_s, flag, i, br)
+        ct, st = tiled(ct, sw), tiled(st, sw)
         q_raw = raw[:, :sw]
         k_raw = raw[:, sw : 2 * sw]
         own_vals = raw[:, 2 * sw :]
         q_rot = (q_raw * ct + rotate_lanes(q_raw, first) * st).astype(BF)
         qo[rows, :] = (q_rot.astype(F32) * HEAD_DIM**-0.5).astype(BF)
         ko[rows, :] = (k_raw * ct + rotate_lanes(k_raw, first) * st).astype(BF)
-        mo[rows, :] = (0.5 * own_vals + 0.5 * va[rows, :].astype(F32)).astype(BF)
+        own_rows[rows, :] = own_vals
         own[...] += jnp.sum((own_vals * own_vals).reshape(br // 8, 8, sw), axis=0)
         return carry
 
     lax.fori_loop(0, row_len // br, project, 0)
 
-    bias = bias_ref[0:1, 0:1]
+    for get, put in local:
+        get.wait()
+        put.start()
+    for dq in range(1, nh):
+        t = (nh - dq) % nh
+        remote(cross, g2.at[h, t], gp_s.at[dq], gp_r.at[dq], mate).wait_recv()
+        for dh in range(1, hi_n):
+            shard_hi(g2.at[h, t], dh, t).start()
+
+    for b in range(n):
+        @pl.when(jnp.logical_or(other, p != b))
+        def _():
+            remote(columns_of(v, 0, sw), va.at[b], v_s.at[b], v_r.at[b], mate).wait_recv()
+
+    @pl.when(c == r)
+    def _():
+        keep_v.wait()
+
+    for b in range(n):
+        rows = pl.ds(b * tok, tok)
+        mo[rows, :] = (0.5 * own_rows[rows, :] + 0.5 * va[b].astype(F32)).astype(BF)
+
+    bias = flag * -1e30
     blocks = row_len // block
     per = block // tok
     causal = lax.broadcasted_iota(jnp.int32, (block, block), 0) >= lax.broadcasted_iota(
@@ -392,20 +545,46 @@
 
     lax.fori_loop(0, pairs, drain, 0)
 
-
-def attention_forward(sizes, xa, ws, va, g1, cos, sin, bias):
-    _, _, _, nh = sizes
+    for s in range(n):
+        @pl.when(jnp.logical_or(other, p != s))
+        def _():
+            send_v(s).wait_send()
+
+    for dq in range(1, nh):
+        shard_peer(dq).wait_send()
+    for dh in range(1, hi_n):
+        rows_hi(dh).wait_send()
+        remote(oz, oh.at[from_hi(dh)], oh_s.at[dh], oh_r.at[dh], mate).wait_recv()
+        for t in range(nh):
+            shard_hi(cross, dh, t).wait_send()
+            remote(cross, g2.at[from_hi(dh), t], gh_s.at[dh, t], gh_r.at[dh, t], mate).wait_recv()
+
+    @pl.when(other)
+    def _():
+        send_dy().wait_send()
+        send_dy().wait_recv()
+
+    for _, put in local:
+        put.wait()
+
+
+def attention_forward(sizes, v, gout, cross, oz, xa, ws, g1, tables, seg):
+    hi_n, _, _, nh = sizes
     n = 2 * nh
-    row_len, sw = va.shape
+    row_len, width = xa.shape
+    sw = ws.shape[0] // 3
     tok = row_len // n
-    pw = cos.shape[1]
+    pw = tables[0].shape[1]
     pairs = sw // pw
     block = max(tok, 512)
-    flops = 2 * row_len * xa.shape[1] * 3 * sw + 2 * row_len * row_len * sw
+    flops = 2 * row_len * width * 3 * sw + 2 * row_len * row_len * sw
     return pl.pallas_call(
         functools.partial(forward_kernel, sizes, block),
         out_shape=(
             jax.ShapeDtypeStruct((n, tok, sw), BF),
+            jax.ShapeDtypeStruct((tok, width), BF),
+            jax.ShapeDtypeStruct((hi_n, nh) + cross.shape, BF),
+            jax.ShapeDtypeStruct((hi_n,) + oz.shape, BF),
             jax.ShapeDtypeStruct((row_len, sw), BF),
             jax.ShapeDtypeStruct((row_len, sw), BF),
             jax.ShapeDtypeStruct((row_len, sw), BF),
@@ -413,9 +592,21 @@
             jax.ShapeDtypeStruct((pairs, row_len, pw // HEAD_DIM), F32),
             jax.ShapeDtypeStruct((8, sw), F32),
         ),
-        in_specs=[VM] * 7,
-        out_specs=(ANY,) + (VM,) * 6,
-        scratch_shapes=[DMA((pairs, n)), DMA((pairs, n)), DMA((pairs,))],
+        in_specs=[ANY] * 4 + [VM] * 8,
+        out_specs=(ANY,) * 4 + (VM,) * 6,
+        scratch_shapes=[
+            pltpu.VMEM((n, tok, sw), BF),
+            pltpu.VMEM((row_len, sw), F32),
+            pltpu.VMEM(cross.shape, BF),
+            pltpu.VMEM(oz.shape, BF),
+            DMA((pairs, n)), DMA((pairs, n)), DMA((pairs,)),
+            DMA((n,)), DMA((n,)),
+            DMA, DMA,
+            DMA((nh,)), DMA((nh,)),
+            DMA((hi_n, nh)), DMA((hi_n, nh)),
+            DMA((hi_n,)), DMA((hi_n,)),
+            DMA((5,)),
+        ],
         name="attention_forward",
         compiler_params=pltpu.CompilerParams(
             collective_id=2, has_side_effects=True, vmem_limit_bytes=VMEM_MAX
@@ -423,21 +614,41 @@
         cost_estimate=pl.CostEstimate(
             flops=4 * flops, bytes_accessed=16 << 20, transcendentals=row_len * row_len * sw // 128
         ),
-    )(xa, ws, va, g1, cos, sin, bias)
+    )(v, gout, cross, oz, xa, ws, g1, *tables, seg)
 
 
 def mlp_kernel(
-    xa, ai, dy, g2, wo, wm, lo, gh, ga, dsum, dosum, gg2,
-    x, hid, n2, acc_o, acc_g, buf, rcv, bo, rcvo, x_s, buf_s, buf_r, bo_s, bo_r,
+    xa, gout, dy_in, near, far, oh, ai, g2, lo, gh, ga, dsum, dosum, gg2, theirs,
+    x, dy, hid, n2, acc_o, acc_g, buf, rcv, bo, rcvo, wm, wo, oa, ob,
+    x_s, buf_s, buf_r, bo_s, bo_r, ld, th_s, th_r, o_s, o_r,
 ):
     step = pl.program_id(0)
     n = ai.shape[0]
-    wide = wm.shape[0]
+    nh = n // 2
+    hi_n = wm.shape[2]
+    wide = 2 * hi_n
     width = x.shape[1]
     dw = width // wide
-    hi_n = wide // 2
     rw = bo.shape[3]
     h, c, r, q = coords()
+    own_dy = pltpu.make_async_copy(gout, dy, ld.at[4])
+    swapped_dy = pltpu.make_async_copy(dy_in, dy, ld.at[4])
+    own_o = pltpu.make_async_copy(oh, oa, ld.at[5])
+
+    def block_of(t):
+        return near.at[:, t] if t < nh else far.at[:, t - nh]
+
+    def give(t):
+        return remote(block_of(t), theirs.at[t], th_s.at[t], th_r.at[t], (h, 1 - c, r, q))
+
+    def give_o():
+        return remote(oh, ob, o_s, o_r, (h, 1 - c, r, q))
+
+    def load_own(src, at):
+        return pltpu.make_async_copy(src, wm.at[at, c], ld.at[at])
+
+    def load_theirs(t, at):
+        return pltpu.make_async_copy(theirs.at[t], wm.at[at, 1 - c], ld.at[2 + at])
     own_x = pltpu.make_async_copy(xa.at[c * (n // 2) + q], x, x_s)
     mate = (h, 1 - c, r, q)
     slot = step % 2
@@ -452,10 +663,32 @@
     @pl.when(step == 0)
     def _():
         own_x.start()
+        own_o.start()
+        load_own(near.at[:, 0], 0).start()
+
+        @pl.when(c == r)
+        def _():
+            own_dy.start()
+
+        @pl.when(c != r)
+        def _():
+            swapped_dy.start()
+
         barrier = pltpu.get_barrier_semaphore()
         pl.semaphore_signal(barrier, inc=1, device_id=mate, device_id_type=MESH)
         pl.semaphore_wait(barrier, 1)
+        give_o().start()
+        for t in range(n):
+            give(t).start()
         own_x.wait()
+        own_o.wait()
+        own_dy.wait()
+        give_o().wait_recv()
+        for s in range(n):
+            for w in range(wide):
+                wo[s, w * rw : (w + 1) * rw] = jnp.where(c == w % 2, oa[w // 2, s], ob[w // 2, s])
+        give(0).wait_recv()
+        load_theirs(0, 0).start()
         total = x[...].astype(F32)
         for s in range(n):
             total = total + nn(ai[s], wo[s])
@@ -471,8 +704,11 @@
         def _():
             to_mate(slot).wait_send()
 
+        load_own(near.at[:, 0], slot).wait()
+        load_theirs(0, slot).wait()
+
         def weight(j):
-            return jnp.concatenate([wm[w, 0, j] for w in range(wide)], axis=1)
+            return jnp.concatenate([wm[slot, w % 2, w // 2, j] for w in range(wide)], axis=1)
 
         def put(j, grad):
             low = grad.astype(BF)
@@ -485,6 +721,13 @@
         silu = gate * sig
         inner = (silu * up).astype(BF)
         grad_inner = nt(dy[...], weight(2))
+        for t in range(1, n):
+            @pl.when(step == t - 1)
+            def _():
+                load_own(block_of(t), t % 2).start()
+                give(t).wait_recv()
+                load_theirs(t, t % 2).start()
+
         grad_gate = (grad_inner * up * sig * (1.0 + gate * (1.0 - sig))).astype(BF)
         grad_up = (grad_inner * silu).astype(BF)
         acc_o[...] += nn(inner, weight(2))
@@ -537,15 +780,17 @@
                 dosum[a, s] = total.astype(BF)
         out_to_mate().wait_send()
         to_mate(0).wait_send()
-        if n > 1:
-            to_mate(1).wait_send()
-
-
-def feed_forward(xa, ai, dy, g2, wo, wm):
+        to_mate(1).wait_send()
+        give_o().wait_send()
+        for t in range(n):
+            give(t).wait_send()
+
+
+def feed_forward(xa, gout, dy_in, near, far, oh, ai, g2):
     n, tok, sw = ai.shape
-    width = dy.shape[1]
-    wide, _, _, ffs, dw = wm.shape
-    hi_n = wide // 2
+    width = gout.shape[1]
+    hi_n, _, _, ffs, dw = near.shape
+    wide = 2 * hi_n
     rw = sw // wide
 
     def whole(*shape):
@@ -565,19 +810,11 @@
             jax.ShapeDtypeStruct((hi_n, n, 3, ffs, dw), BF),
             jax.ShapeDtypeStruct((hi_n, n, rw, width), BF),
             jax.ShapeDtypeStruct((8, width), F32),
+            jax.ShapeDtypeStruct((n, hi_n, 3, ffs, dw), BF),
         ),
         grid_spec=pl.GridSpec(
             grid=(n + 1,),
-            in_specs=[
-                ANY,
-                fixed(n, tok, sw),
-                fixed(tok, width),
-                fixed(1, width),
-                fixed(n, sw, width),
-                pl.BlockSpec(
-                    (wide, 1, 3, ffs, dw), lambda i: (0, jnp.minimum(i, n - 1), 0, 0, 0)
-                ),
-            ],
+            in_specs=[ANY] * 6 + [fixed(n, tok, sw), fixed(1, width)],
             out_specs=(
                 whole(tok, width),
                 whole(tok, width),
@@ -587,8 +824,10 @@
                 ),
                 whole(hi_n, n, rw, width),
                 whole(8, width),
+                ANY,
             ),
             scratch_shapes=[
+                pltpu.VMEM((tok, width), BF),
                 pltpu.VMEM((tok, width), BF),
                 pltpu.VMEM((tok, width), F32),
                 pltpu.VMEM((tok, width), BF),
@@ -598,7 +837,12 @@
                 pltpu.VMEM((2, hi_n, 3, ffs, dw), BF),
                 pltpu.VMEM((2, hi_n, n, rw, width), BF),
                 pltpu.VMEM((hi_n, n, rw, width), BF),
+                pltpu.VMEM((2, 2, hi_n, 3, ffs, dw), BF),
+                pltpu.VMEM((n, sw, width), BF),
+                pltpu.VMEM((hi_n, n, rw, width), BF),
+                pltpu.VMEM((hi_n, n, rw, width), BF),
                 DMA, DMA((2,)), DMA((2,)), DMA, DMA,
+                DMA((6,)), DMA((n,)), DMA((n,)), DMA, DMA,
             ],
         ),
         name="feed_forward",
@@ -611,15 +855,15 @@
         cost_estimate=pl.CostEstimate(
             flops=18 * tok * width * ffs * n, bytes_accessed=40 << 20, transcendentals=tok * ffs * n
         ),
-    )(xa, ai, dy, g2, wo, wm)
+    )(xa, gout, dy_in, near, far, oh, ai, g2)
 
 
 def backward_kernel(
-    sizes, block, ga, ds, dos, lo, xa, ws, g1, cos, sin, bias_ref, qi, ki, mi, ao, lse, gh,
+    sizes, block, ga, ds, dos, lo, xa, ws, g1, lo_c, lo_s, hi_c, hi_s, seg, qi, ki, mi, ao, lse, gh,
     gv, gi, dwq, gg1, lo_in, rx, rxo, zr, zo,
     do, normed, dq, dk, dv, dcat, gow, gnp, rcv, rcv2, gis, part, zs, zos, do_part,
     do_s, do_r, gv_s, gv_r, co_s, co_r, pe_s, pe_r, gi_s, gi_r, loc,
-    rx_s, rx_r, rxo_s, rxo_r, lo_s, lo_r, ld, z_s, z_r, zo_s, zo_r,
+    rx_s, rx_r, rxo_s, rxo_r, ly_s, ly_r, ld, z_s, z_r, zo_s, zo_r,
 ):
     hi_n, _, _, nh = sizes
     n = 2 * nh
@@ -629,7 +873,7 @@
     width = xa.shape[1]
     tok = row_len // n
     short = row_len // 2
-    pw = cos.shape[1]
+    pw = lo_c.shape[1]
     pairs = sw // pw
     halves = pw // HEAD_DIM
     same = c == r
@@ -649,16 +893,17 @@
         return remote(dos.at[to], rxo.at[dh - 1], rxo_s.at[dh], rxo_r.at[dh], (to, c, r, q))
 
     def send_lo():
-        return remote(lo, lo_in, lo_s, lo_r, swap_to)
-
-    def over_z(i):
-        return remote(zs.at[i], zr.at[zed], z_s.at[i], z_r.at[zed], (h, c, i // nh, i % nh))
+        return remote(lo, lo_in, ly_s, ly_r, swap_to)
+
+    def over_z(t):
+        to = (h, c, (r + t // nh) % 2, (q + t % nh) % nh)
+        return remote(zs.at[t], zr.at[zed], z_s.at[t], z_r.at[zed], to)
 
     def out_over_z(i):
         return remote(zos.at[i], zo.at[zed], zo_s.at[i], zo_r.at[zed], (h, c, i // nh, i % nh))
 
-    def keep_z(i):
-        return pltpu.make_async_copy(zs.at[i], zr.at[i], z_s.at[i])
+    def keep_z():
+        return pltpu.make_async_copy(zs.at[0], zr.at[zed], z_s.at[0])
 
     def keep_out_z(i):
         return pltpu.make_async_copy(zos.at[i], zo.at[i], zo_s.at[i])
@@ -682,13 +927,10 @@
                 total = total + part[dh, j].astype(F32)
             zs[i, j] = total.astype(BF)
 
-        @pl.when(zed != i)
-        def _():
+        if i:
             over_z(i).start()
-
-        @pl.when(zed == i)
-        def _():
-            keep_z(i).start()
+        else:
+            keep_z().start()
 
     own_out = pltpu.make_async_copy(dos.at[h], zos, ld.at[0])
 
@@ -748,23 +990,29 @@
             remote(ga.at[s], do.at[s], do_s.at[s], do_r.at[s], mate).wait_recv()
             send_do(s).wait_send()
 
-    bias = bias_ref[0:1, 0:1]
+    flag = seg[0:1, 0:1]
+    bias = flag * -1e30
     blocks = row_len // block
     per = block // tok
     causal = lax.broadcasted_iota(jnp.int32, (block, block), 0) >= lax.broadcasted_iota(
         jnp.int32, (block, block), 1
     )
 
+    def gv_at(s, pair):
+        if len(gv.shape) == 3:
+            return gv.at[s]
+        return gv.at[:, pl.ds(pl.multiple_of(s * sw + pair * pw, pw), pw)]
+
     def send_gv(b, pair):
         lanes = lane_window(pair, pw, sw)
         to = (h, r, b // nh, b % nh)
         return remote(
-            gow.at[b, :, lanes], gv.at[p, :, lanes], gv_s.at[pair, b], gv_r.at[pair, p], to
+            gow.at[b, :, lanes], gv_at(p, pair), gv_s.at[pair, b], gv_r.at[pair, p], to
         )
 
     def keep_gv(pair):
         lanes = lane_window(pair, pw, sw)
-        return pltpu.make_async_copy(gow.at[p, :, lanes], gv.at[p, :, lanes], loc.at[1 + pair])
+        return pltpu.make_async_copy(gow.at[p, :, lanes], gv_at(p, pair), loc.at[1 + pair])
 
     def pair_step(pair, carry):
         lanes = lane_window(pair, pw, sw)
@@ -810,8 +1058,7 @@
 
         def finish(i, inner_carry):
             rows = pl.ds(pl.multiple_of(i * br, br), br)
-            ct = cos[rows, :]
-            st = sin[rows, :]
+            ct, st = rope_rows(lo_c, lo_s, hi_c, hi_s, flag, i, br)
             a = dq[rows, :]
             b = dk[rows, :]
             dcat[0, rows, lanes] = (a * ct - rotate_lanes(a, first) * st).astype(BF)
@@ -949,7 +1196,7 @@
             def _():
                 send_gv(b, pair).wait_send()
                 remote(
-                    gow.at[b, :, lanes], gv.at[b, :, lanes], gv_s.at[pair, b], gv_r.at[pair, b], mate
+                    gow.at[b, :, lanes], gv_at(b, pair), gv_s.at[pair, b], gv_r.at[pair, b], mate
                 ).wait_recv()
 
         @pl.when(same)
@@ -972,22 +1219,24 @@
     for i in range(n):
         @pl.when(zed != i)
         def _():
-            over_z(i).wait_send()
             out_over_z(i).wait_send()
             remote(zs.at[i], zr.at[i], z_s.at[i], z_r.at[i], mate).wait_recv()
             remote(zos.at[i], zo.at[i], zo_s.at[i], zo_r.at[i], mate).wait_recv()
 
         @pl.when(zed == i)
         def _():
-            keep_z(i).wait()
             keep_out_z(i).wait()
 
-
-def attention_backward(sizes, ga, ds, dos, lo, xa, ws, g1, cos, sin, bias, qi, ki, mi, ao, lse, gh):
+    keep_z().wait()
+    for t in range(1, n):
+        over_z(t).wait_send()
+
+
+def attention_backward(sizes, ga, ds, dos, lo, xa, ws, g1, tables, seg, qi, ki, mi, ao, lse, gh):
     _, _, _, nh = sizes
     n, tok, sw = ga.shape
     row_len, width = xa.shape
-    pw = cos.shape[1]
+    pw = tables[0].shape[1]
     pairs = sw // pw
     block = max(tok, 512)
     ck = min(256, tok)
@@ -1000,7 +1249,7 @@
     return pl.pallas_call(
         functools.partial(backward_kernel, sizes, block),
         out_shape=(
-            jax.ShapeDtypeStruct((n, tok, sw), BF),
+            jax.ShapeDtypeStruct((n, tok, sw) if sw % 128 else (tok, width), BF),
             jax.ShapeDtypeStruct((tok, width), BF),
             jax.ShapeDtypeStruct((3 * sw, width), BF),
             jax.ShapeDtypeStruct((8, width), F32),
@@ -1010,7 +1259,7 @@
             jax.ShapeDtypeStruct((n, 3, ffs, dw), BF),
             jax.ShapeDtypeStruct((n, rw, width), BF),
         ),
-        in_specs=[ANY] * 4 + [VM] * 12,
+        in_specs=[ANY] * 4 + [VM] * 14,
         out_specs=(ANY, ANY, VM, VM) + (ANY,) * 5,
         scratch_shapes=[
             pltpu.VMEM((n, tok, sw), BF),
@@ -1048,7 +1297,7 @@
         cost_estimate=pl.CostEstimate(
             flops=60 << 30, bytes_accessed=24 << 20, transcendentals=row_len * row_len * sw // 128
         ),
-    )(ga, ds, dos, lo, xa, ws, g1, cos, sin, bias, qi, ki, mi, ao, lse, gh)
+    )(ga, ds, dos, lo, xa, ws, g1, *tables, seg, qi, ki, mi, ao, lse, gh)
 
 
 def finish_kernel(
@@ -1237,53 +1486,27 @@
     wide = 2 * hi_n
     tok, width = layer_in.shape
     sw = w_qkv.shape[1]
-    ffs = w_mlp.shape[2]
-    dw = w_mlp.shape[0]
     row_len = n * tok
-    short = row_len // seg_start.shape[0]
     h, c, r, q = coords()
 
-    w_mlp_t = jnp.transpose(w_mlp, (1, 2, 0)).reshape(3 * ffs, dw)
-    wm = lax.all_gather(w_mlp_t, AXES, axis=0, tiled=False).reshape(wide, n, 3, ffs, dw)
-    wo = lax.all_gather(w_out, ("zh", "zq"), axis=0, tiled=False)
-
-    swap = [
-        (((a * 2 + b) * 2 + d) * nh + e, ((a * 2 + d) * 2 + b) * nh + e)
-        for a in range(hi_n)
-        for b in range(2)
-        for d in range(2)
-        for e in range(nh)
-    ]
-    v_cut = value_first.reshape(tok, n, sw).transpose(1, 0, 2)
+    w_mlp_t = jnp.transpose(w_mlp, (1, 2, 0))
     sg = jnp.full((8, 128), seg_start[1].astype(F32))
     w_cut = w_qkv.reshape(hi_n, 3 * sw // hi_n, width)
-    xa, va, ws, so = exchange_inputs(sizes, layer_in, v_cut, w_cut, sg)
+    wo_cut = w_out.reshape(wide, sw // wide, width)
+    v_cut = value_first.reshape(tok, n, sw).transpose(1, 0, 2) if sw % 128 else value_first
+    xa, ws, so, near, cross, oz = exchange_inputs(sizes, layer_in, w_cut, sg, w_mlp_t, wo_cut)
     ws = ws.reshape(3 * sw, width)
-    dy = lax.ppermute(grad_out, AXES, swap)
-
-    joined = 1.0 - so[0, 0]
-    index = jnp.arange(row_len, dtype=jnp.int32)
-    slot = index // short
-    positions = (index - slot * short).astype(F32) + jnp.where(slot == 1, joined * short, 0.0)
-    pw = min(sw, 128)
-    half_dim = HEAD_DIM // 2
-    frequency = 10000.0 ** (-2.0 * jnp.arange(half_dim, dtype=F32) / HEAD_DIM)
-    angles = positions[:, None] * frequency[None, :]
-    cosine, sine = jnp.cos(angles), jnp.sin(angles)
-    times = pw // HEAD_DIM
-    cos = jnp.concatenate([cosine, cosine] * times, axis=1)
-    sin = jnp.concatenate([-sine, sine] * times, axis=1)
-    bias = (1.0 - joined) * jnp.full((8, 128), -1e30, F32)
-
+
+    tables = rope_parts(row_len, min(sw, 128))
     g1 = gain_one.reshape(1, width)
     g2 = gain_two.reshape(1, width)
     xr = xa.reshape(row_len, width)
-    ai, qo, ko, mo, ao, lse, own = attention_forward(
-        sizes, xr, ws, va.reshape(row_len, sw), g1, cos, sin, bias
+    ai, dy_in, far, oh, qo, ko, mo, ao, lse, own = attention_forward(
+        sizes, v_cut, grad_out, cross, oz, xr, ws, g1, tables, so
     )
-    lo, gh, ga, ds, dos, gg2 = feed_forward(xa, ai, dy, g2, wo, wm)
+    lo, gh, ga, ds, dos, gg2, _ = feed_forward(xa, grad_out, dy_in, near, far, oh, ai, g2)
     gv, gi, dwq, gg1, lo_in, _, _, zr, zo = attention_backward(
-        sizes, ga, ds, dos, lo, xr, ws, g1, cos, sin, bias, qo, ko, mo, ao, lse, gh
+        sizes, ga, ds, dos, lo, xr, ws, g1, tables, so, qo, ko, mo, ao, lse, gh
     )
     first_f = value_first.astype(F32)
     lane = jnp.arange(width)
@@ -1294,7 +1517,7 @@
     fin, og, sums = finish(sizes, dwq.reshape(hi_n, 3 * sw // hi_n, width), small, zo)
 
     layer_out = jnp.where(c == r, lo, lo_in)
-    grad_value_first = gv.transpose(1, 0, 2).reshape(tok, width).astype(F32)
+    grad_value_first = (gv.transpose(1, 0, 2).reshape(tok, width) if sw % 128 else gv).astype(F32)
     grad_in = gi.astype(F32)
     grad_w_mlp = jnp.transpose(jnp.sum(zr.astype(F32), axis=0), (2, 0, 1))
     grad_w_out = og.reshape(sw, width).astype(F32)

time: 537 us -> 455 us (0.85)
  Pallas kernels: 464 us -> 424 us
  between operations: 15.9 us -> 1.81 us
  starting transfers between devices: 9.52 us -> 0 us
  local copies, waits for them, and re-layouts: 13.5 us -> 4.75 us
  other arithmetic: 21.3 us -> 15.2 us
  waiting for transfers between devices: 5.95 us -> 0 us
    pallas_call x1, Pallas kernels: 112 us -> 74.6 us  [exchange_inputs(): pl.pallas_call(functools.partial(exchange_kernel, sizes, chunks), out_sha...]
    pallas_call x1, Pallas kernels: 147 us -> 158 us  [attention_backward(): pl.pallas_call(functools.partial(backward_kernel, sizes, block), out_shap...]
    pallas_call x1, Pallas kernels: 75 us -> 64.9 us  [finish(): pl.pallas_call(functools.partial(finish_kernel, sizes), out_shape=(jax.Sh...]
    ppermute x1 -> x0, starting transfers between devices: 9.45 us -> none  [per_device(): dy = lax.ppermute(grad_out, AXES, swap)]
    pallas_call x1, Pallas kernels: 78 us -> 69.8 us  [attention_forward(): pl.pallas_call(functools.partial(forward_kernel, sizes, block), out_shape...]
  transfers between devices with their start and end apart: 3 -> 0, of which waited for: 1 -> 0; matrix products, arithmetic and copies ran while one was open for 3% -> 0% of each run, Pallas kernels for 36% -> 0%
where the time goes in v3:
time: 455 us; the launch traced here: 446 us
  Pallas kernels  424 us (93%)
  other arithmetic  15.2 us (3%)
  local copies, waits for them, and re-layouts  4.75 us (1%)
    pallas_call x1, Pallas kernels, attention_backward(): pl.pallas_call(functools.partial(backward_kernel, sizes, block), out_shap...  158 us
    pallas_call x1, Pallas kernels, exchange_inputs(): pl.pallas_call(functools.partial(exchange_kernel, sizes, chunks), out_sha...  74.6 us
    pallas_call x1, Pallas kernels, attention_forward(): pl.pallas_call(functools.partial(forward_kernel, sizes, block), out_shape...  69.8 us
    pallas_call x1, Pallas kernels, finish(): pl.pallas_call(functools.partial(finish_kernel, sizes), out_shape=(jax.Sh...  64.9 us
    pallas_call x1, Pallas kernels, feed_forward(): pl.pallas_call(mlp_kernel, out_shape=(jax.ShapeDtypeStruct((tok, width),...  56.7 us

profile of v3, /device:TPU:0, one launch (start us, length us, event | category | flops | bytes accessed | tf_op | source)
XLA Modules:
  0.0 446.0 jit_solution(10186186675794718854)
XLA Ops:
  0.6 1.2 slice.12
  2.5 0.6 broadcast_in_dim.15.sg
  3.1 74.6 %exchange_inputs.1 = (bf16[4,512,1024]{2,1,0:T(8,128)(2,1)}, bf16[4,192,1024]{2,1,0:T(8,128)(2,1)}, f32[8,128]{1,0:T(8,128)}, bf16[4,2,3,704,128]{4,3,2,1,0:T(8,...) custom-call(bf16[512,1024]{1,0:T(8,128)(2,1)} %x.1, bf16[4,192,1024]{2,1,0:T(8,128)(2,1)} %bitcast.21, ...), custom_call_target="tpu_custom_call" | custom-call | bytes 167772160 | tf_op jit(solution)/shard_map/exchange_inputs/pallas_call | solution.py:315
  77.8 69.8 %attention_forward.1 = (bf16[4,512,256]{2,1,0:T(8,128)(2,1)}, bf16[512,1024]{1,0:T(8,128)(2,1)}, bf16[4,2,3,704,128]{4,3,2,1,0:T(8,128)(2,1)}, bf16[4,4,32,1024]...) custom-call(bf16[512,1024]{1,0:T(8,128)(2,1)} %v.1, ...), custom_call_target="tpu_custom_call" | custom-call | flops 21474836480 | bytes 16777216 | tf_op jit(solution)/shard_map/attention_forward/pallas_call | solution.py:581
  147.6 56.7 %feed_forward.1 = (bf16[512,1024]{1,0:T(8,128)(2,1)}, f32[512,1024]{1,0:T(8,128)}, bf16[4,512,256]{2,1,0:T(8,128)(2,1)}, bf16[4,4,3,704,128]{4,3,2,1,0:T(8,128)(...) custom-call(bf16[4,512,1024]{2,1,0:T(8,128)(2,1)} %get-tuple-element.41.xa, ...), custom_call_target="tpu_custom_call" | custom-call | flops 26575110144 | bytes 41943040 | tf_op jit(solution)/shard_map/feed_forward/pallas_call | solution.py:804
  204.3 0.0 copy-start.7
  204.3 0.0 copy-start.8
  204.4 0.0 copy-start.3
  204.4 158.1 %attention_backward.1 = (bf16[512,1024]{1,0:T(8,128)(2,1)}, bf16[512,1024]{1,0:T(8,128)(2,1)}, bf16[768,1024]{1,0:T(8,128)(2,1)}, f32[8,1024]{1,0:T(8,128)}, bf1...) custom-call(bf16[4,512,256]{2,1,0:T(8,128)(2,1)} %get-tuple-element., ...), custom_call_target="tpu_custom_call" | custom-call | flops 64424509440 | bytes 25165824 | tf_op jit(solution)/shard_map/attention_backward/pallas_call | solution.py:1249
  362.5 0.8 reduce_sum.45
  363.2 0.0 copy-done.7
  363.3 0.0 copy-done.8
  363.3 0.6 reduce_sum.48
  363.9 0.0 copy-done.3
  363.9 1.1 multiply_reduce_fusion
  365.0 1.3 compare_select_fusion.1
  366.3 0.7 stack.16.sm
  367.0 64.9 %finish.1 = (bf16[4,192,1024]{2,1,0:T(8,128)(2,1)}, bf16[8,32,1024]{2,1,0:T(8,128)(2,1)}, f32[8,1024]{1,0:T(8,128)}) custom-call(bf16[4,192,1024]{2,1,0:T(8,128)(2,1)} %bitcast.22, f32[8,1024]{1,0:T(8,128)} %stack.16.sm, bf16[4,32,1024]{2,1,0:T(8,128)(2,1)} %get-tuple-element.68.zo), custom_call_target="tpu_custom_call" | custom-call | tf_op jit(solution)/shard_map/finish/pallas_call | solution.py:1452
  431.9 0.0 copy-start.6
  431.9 0.0 copy-start.2
  431.9 3.6 convert.2
  435.5 0.0 copy-done.6
  435.5 0.0 copy-start.1
  435.5 1.1 bitcast_convert_fusion
  436.6 1.4 fusion
  438.1 1.2 sqrt_bitcast_fusion
  439.3 0.0 copy-done.2
  439.3 1.6 convert_element_type.32
  440.8 0.0 copy-start
  440.8 0.0 copy-done.1
  440.8 1.6 convert_element_type.33
  442.4 0.0 copy-start.4
  442.4 0.0 copy-start.5
  442.4 0.8 copy-done
  443.2 1.3 convert_reduce_fusion
  444.5 0.0 copy-done.4
  444.5 0.0 copy-done.5
  444.5 1.1 broadcast_select_fusion
  (3 shorter events, 0.0 us)
Async XLA Ops:
  204.3 158.9 %copy-start.7 = (f32[8,1024]{1,0:T(8,128)S(1)}, f32[8,1024]{1,0:T(8,128)}, u32[]{:S(2)}) copy-start(f32[8,1024]{1,0:T(8,128)} %get-tuple-element.66) | copy-start | bytes 98308
  204.3 158.9 %copy-start.8 = (f32[8,256]{1,0:T(8,128)S(1)}, f32[8,256]{1,0:T(8,128)}, u32[]{:S(2)}) copy-start(f32[8,256]{1,0:T(8,128)} %get-tuple-element.67) | copy-start | bytes 24580
  204.4 159.5 %copy-start.3 = (bf16[512,1024]{1,0:T(8,128)(2,1)S(1)}, bf16[512,1024]{1,0:T(8,128)(2,1)}, u32[]{:S(2)}) copy-start(bf16[512,1024]{1,0:T(8,128)(2,1)} %v.1) | copy-start | bytes 3145732
  431.9 3.6 copy-start.6
  431.9 7.3 %copy-start.2 = (bf16[512,1024]{1,0:T(8,128)(2,1)S(1)}, bf16[512,1024]{1,0:T(8,128)(2,1)}, u32[]{:S(2)}) copy-start(bf16[512,1024]{1,0:T(8,128)(2,1)} %get-tuple-element.62) | copy-start | bytes 3145732
  435.5 5.3 %copy-start.1 = (bf16[512,1024]{1,0:T(8,128)(2,1)S(1)}, bf16[512,1024]{1,0:T(8,128)(2,1)}, u32[]{:S(2)}) copy-start(bf16[512,1024]{1,0:T(8,128)(2,1)} %get-tuple-element.63) | copy-start | bytes 3145732
  440.8 2.4 copy-start
  442.4 2.1 copy-start.4
  442.4 2.1 copy-start.5
